TPU v7x, 32 devices: a whole 2x2x4 slice. The times are simulated.
32 devices in a mesh: fields: 2 (over x), prow: 8 (over z, y), pcol: 2 (over core).
Axes of the slice: x: 2, y: 2, z: 4, core: 2. Of those that a mesh axis runs over, the one named last changes fastest.
Arguments:
- inverse_tiles: bfloat16 [32, 16, 256, 256], P(('fields', 'prow'), 'pcol'), parts along dimension 0, may hold values from -6 to 6
- panel_blocks: bfloat16 [4, 8, 256, 512], P('fields', 'prow', None, 'pcol'), parts along dimension 0, may hold values from -0.125 to 0.125
- diag_inverse: float32 [4, 512], P('fields', 'pcol'), parts along dimension 0, may hold values from 0.5 to 2
- structure: int32 [4, 8], P('fields'), parts along dimension 0, may hold values from 0 to 15, as said below
- block_slot: int32 [32], P('fields'), parts along dimension 0, may hold values from 0 to 15, each once
Outputs:
- sigma_new: bfloat16 [4, 16, 256, 512], P('fields', 'prow', None, 'pcol'), parts along dimension 0
- variances: float32 [4, 512], P('fields', 'pcol'), parts along dimension 0
There are 2 independent parts, one for each index of `fields`. A program takes and returns all parts, laid end to end along the dimension named above; each array names one. Nothing has to cross between parts.
Inputs may be any that keep to these rules, and one draw needn't show every extreme that they name: `structure`: each row lists 8 distinct row blocks in increasing order, and the last is always 16 - 1. `block_slot`: each slot is used by exactly one row block.
All inputs are finite; a program needn't handle non-finite values.
Results may differ from a plain program's by a relative error of at most 0.0006.
Values may be sent and summed in bfloat16 or wider, within the bound.
No kernel may reach another device: no remote copies, remote signals or barrier semaphores. Data moves between devices by JAX's collectives and lax.ppermute only.
A program may use at most 128 MiB of HBM per device.

v0:
```python
import jax
import jax.numpy as jnp
from jax import lax
from jax.sharding import PartitionSpec as P


def swapped(shard, axis, stride):
    return lax.ppermute(shard, axis, [(i, i ^ 1 << stride) for i in range(lax.axis_size(axis))])


def make_accumulate(selected, row_hits, piece):
    contrib = jnp.einsum("iskxy,skyw->sixw", selected, piece, preferred_element_type=jnp.float32)
    own_panel = jnp.einsum("sik,skxw->sixw", row_hits, piece, preferred_element_type=jnp.float32)
    return (contrib, own_panel)


def per_device(inverse_tiles, panel_blocks, diag_inverse, structure, block_slot):
    rows_here = inverse_tiles.shape[0]
    tile_size = inverse_tiles.shape[2]
    supernodes = panel_blocks.shape[0]
    positions = structure.shape[1]
    prow_index = lax.axis_index("prow")
    pcol_index = lax.axis_index("pcol")
    slot_of = block_slot[structure]
    own_rows = prow_index * rows_here + jnp.arange(rows_here, dtype=jnp.int32)
    row_match = slot_of[:, None, :] == own_rows[None, :, None]
    row_hits = row_match.astype(jnp.bfloat16)
    row_used = jnp.any(row_match, axis=2)
    partner = swapped(inverse_tiles, "pcol", 0)
    first_half = jnp.where(pcol_index == 0, inverse_tiles, partner)
    second_half = jnp.where(pcol_index == 0, partner, inverse_tiles)
    whole_rows = jnp.concatenate([first_half, second_half], axis=1)
    selected = jnp.take(whole_rows, slot_of.reshape(-1), axis=1)
    selected = selected.reshape(rows_here, supernodes, positions, tile_size, tile_size)
    summed, own_panel = make_accumulate(
        selected, row_hits, lax.all_gather(panel_blocks, "prow", axis=1, tiled=True)
    )
    sigma_rows = jnp.where(row_used[:, :, None, None], -summed, jnp.zeros((), jnp.float32))
    partial_value = jnp.sum(own_panel * sigma_rows, axis=(1, 2))
    correction = lax.psum(partial_value, "prow")
    variances = diag_inverse - correction
    return (sigma_rows.astype(jnp.bfloat16), variances)


def solution(mesh):
    in_specs = (
        P(("fields", "prow"), "pcol", None, None),
        P("fields", "prow", None, "pcol"),
        P("fields", "pcol"),
        P("fields", None),
        P("fields"),
    )
    out_specs = (P("fields", "prow", None, "pcol"), P("fields", "pcol"))
    return jax.shard_map(
        per_device, mesh=mesh, in_specs=in_specs, out_specs=out_specs, check_vma=False
    )
```

profile of v0, /device:TPU:0, one launch (start us, length us, event | category | flops | bytes accessed | tf_op | source)
XLA Modules:
  0.0 95.9 jit_solution(17099047433927221169)
XLA Ops:
  7.2 0.0 copy-start
  7.2 0.0 all-gather.2.cloned.1.call-start
  7.2 0.7 all-gather.2.cloned.1.call-update
  7.9 0.6 collective-permute-start
  8.5 0.7 compare_select_fusion.1
  9.2 0.1 reshape.53
  9.2 0.0 copy-done
  9.2 0.7 gather_fusion
  9.9 0.1 reshape.52
  10.0 0.2 compare_reduce_fusion
  10.2 2.3 %collective-permute-done = bf16[2,8,256,256]{3,2,1,0:T(8,128)(2,1)S(1)} collective-permute-done((bf16[2,8,256,256]{3,2,1,0:T(8,128)(2,1)}, bf16[2,8,256,256]{3,2,1,0:T(8,128)(2,1)S(1)}, u32[]{:S(2)}, u32[]{:S(2)}) %collective-permute-start) | collective-permute-done | bytes 2097184 | tf_op jit(solution)/shard_map/ppermute | solution.py:8
  12.5 1.9 %broadcast_select_fusion.1 = (bf16[2,8,256,256]{3,2,1,0:T(8,128)(2,1)S(1)}, bf16[2,8,256,256]{3,2,1,0:T(8,128)(2,1)S(1)}) fusion(bf16[2,8,256,256]{3,2,1,0:T(8,128)(2,1)} %param.5, bf16[2,8,256,256]{3,2,1,0:T(8,128)(2,1)S(1)} %collective-permute-done, pred[]{:T(512)S(6)} %eq.20), kind=kLoop, calls=%fused_computation.11 | loop fusion | flops 2097152 | bytes 8388609 | tf_op jit(solution)/shard_map/jit(_where)/select_n | solution.py:30
  14.3 2.3 %pad_maximum_fusion = bf16[2,16,256,256]{3,2,1,0:T(8,128)(2,1)} fusion(bf16[2,8,256,256]{3,2,1,0:T(8,128)(2,1)S(1)} %get-tuple-element.3, bf16[2,8,256,256]{3,2,1,0:T(8,128)(2,1)S(1)} %get-tuple-element.2), kind=kLoop, calls=%fused_computation.2 | loop fusion | flops 2097152 | bytes 8388608 | tf_op jit(solution)/shard_map/concatenate | solution.py:32
  16.7 4.9 %gather_fusion.1 = bf16[16,2,256,256]{3,2,1,0:T(8,128)(2,1)} fusion(bf16[2,16,256,256]{3,2,1,0:T(8,128)(2,1)} %pad_maximum_fusion, s32[1024]{0:T(1024)S(1)} %pad_clamp_fusion), kind=kCustom, calls=%fused_computation.1 | custom fusion | bytes 8388672 | tf_op jit(solution)/shard_map/jit(_take)/gather | solution.py:33
  21.6 40.4 %all-gather.2.cloned.1.call-done = bf16[2,8,256,256]{3,2,1,0:T(8,128)(2,1)} async-done(((bf16[2,1,256,256]{3,2,1,0:T(8,128)(2,1)}), bf16[2,8,256,256]{3,2,1,0:T(8,128)(2,1)}) %all-gather.2.cloned.1.call-update) | async-done | bytes 2097168 | tf_op jit(solution)/shard_map/all_gather | solution.py:36
  62.0 0.0 copy-start.1
  62.0 3.2 %fusion.3 = f32[2,2,256,256]{3,1,2,0:T(2,128)S(1)} fusion(bf16[2,8,256,256]{3,2,1,0:T(8,128)(2,1)} %all-gather.2.cloned.1.call-done, s32[2,8]{1,0:T(2,128)S(1)} %reshape.52, s32[2]{0:T(128)S(1)} %iota_add_fusion), kind=kOutput, calls=%fused_computation.7 | convolution fusion | flops 4194336 | bytes 3145800 | tf_op jit(solution)/shard_map/sik,skxw->sixw/dot_general | solution.py:13
  65.2 0.0 copy-done.1
  65.2 0.0 copy-start.2
  65.2 4.3 %fusion.15 = (f32[2,256]{1,0:T(2,128)S(1)}, bf16[2,2,256,256]{3,2,1,0:T(8,128)(2,1)}) fusion(f32[2,2,256,256]{3,1,2,0:T(2,128)S(1)} %fusion.3, bf16[2,8,256,256]{3,2,1,0:T(8,128)(2,1)S(1)} %copy-done.1, bf16[2,2,8,256,256]{4,3,0,2,1:T(8,128)(2,1)} %bitcast.32, pred[2,8]{1,0:T(4,128)(4,1)S(1)} %compare_and_fusion, pred[2,2]{1,0:T(4,128)(4,1)S(1)} %compare_reduce_fusion), kind=kOutput, calls=%fused_computation.16 | convolution fusion | flops 1077149184 | bytes 7866388 | tf_op jit(solution)/shard_map/iskxy,skyw->sixw/dot_general | solution.py:12
  69.5 19.0 %psum.7 = f32[2,256]{1,0:T(2,128)S(1)} all-reduce(f32[2,256]{1,0:T(2,128)S(1)} %get-tuple-element.4), channel_id=1, replica_groups=mesh['fields'=2,'prow'=8,'pcol'=2] {'prow'}, use_global_device_ids=true, to_apply=%region_2.3 | all-reduce | flops 512 | bytes 4096 | tf_op jit(solution)/shard_map/psum | solution.py:40
  88.5 0.0 copy-done.2
  88.5 0.6 sub.3
  (5 shorter events, 0.0 us)
Async XLA Ops:
  7.2 2.1 %copy-start = (s32[16]{0:T(128)S(1)}, s32[16]{0:T(128)}, u32[]{:S(2)}) copy-start(s32[16]{0:T(128)} %param.9) | copy-start | bytes 196
  7.2 54.8 %all-gather.2.cloned.1.call-start = ((), (), s32[]{:S(2)}) async-start(), calls=%async_computation | async-start | bytes 2359296 | tf_op jit(solution)/shard_map/all_gather | solution.py:36
  7.9 4.6 %collective-permute-start = (bf16[2,8,256,256]{3,2,1,0:T(8,128)(2,1)}, bf16[2,8,256,256]{3,2,1,0:T(8,128)(2,1)S(1)}, u32[]{:S(2)}, u32[]{:S(2)}) collective-permute-start(bf16[2,8,256,256]{3,2,1,0:T(8,128)(2,1)} %param.5), channel_id=1, source_target_pairs={{0,1},{1,0},{2,3},{3,2},{4,5},{5,4},{6,7},{7,6},{8,9},{9,8},{10,11... | collective-permute-start | bytes 6291464 | tf_op jit(solution)/shard_map/ppermute | solution.py:8
  62.0 3.2 %copy-start.1 = (bf16[2,8,256,256]{3,2,1,0:T(8,128)(2,1)S(1)}, bf16[2,8,256,256]{3,2,1,0:T(8,128)(2,1)}, u32[]{:S(2)}) copy-start(bf16[2,8,256,256]{3,2,1,0:T(8,128)(2,1)} %all-gather.2.cloned.1.call-done) | copy-start | bytes 6291460
  65.2 23.3 %copy-start.2 = (f32[2,256]{1,0:T(2,128)S(1)}, f32[2,256]{1,0:T(2,128)}, u32[]{:S(2)}) copy-start(f32[2,256]{1,0:T(2,128)} %param.7) | copy-start | bytes 6148
Sparse Core Ops, SparseCore 0:
  10.2 51.7 all-gather.1
where the time goes:
time: 96.1 us; the launch traced here: 95.9 us
  waiting for transfers between devices  43.3 us (45%)
  blocking collectives  19 us (20%)
  between operations  14.1 us (15%)
  matrix products  7.51 us (8%)
  local copies, waits for them, and re-layouts  5.78 us (6%)
  other arithmetic  5.67 us (6%)
    all_gather x1, waiting for transfers between devices, per_device(): lax.all_gather(panel_blocks, 'prow', axis=1, tiled=True)  40.4 us
    psum x1, blocking collectives, per_device(): correction = lax.psum(partial_value, 'prow')  19 us
    gather x1, local copies, waits for them, and re-layouts, per_device(): selected = jnp.take(whole_rows, slot_of.reshape(-1), axis=1)  4.94 us
    dot_general x1, matrix products, make_accumulate(): jnp.einsum('iskxy,skyw->sixw', selected, piece, preferred_element_type=jn...  4.32 us
    dot_general x1, matrix products, make_accumulate(): jnp.einsum('sik,skxw->sixw', row_hits, piece, preferred_element_type=jnp....  3.19 us
    concatenate x1, other arithmetic, per_device(): whole_rows = jnp.concatenate([first_half, second_half], axis=1)  2.33 us
    ppermute x1, waiting for transfers between devices, swapped(): lax.ppermute(shard, axis, [(i, i ^ 1 << stride) for i in range(lax.axis_s...  2.26 us
  transfers between devices with their start and end apart: 2, of which 2 were waited for; matrix products, arithmetic and copies ran while one was open for 11% of the time, Pallas kernels for 0%

commit v1 on v0

v1 whole, which is shorter than its diff:
```python
import functools
import jax
import jax.numpy as jnp
from jax import lax
from jax.experimental import pallas as pl
from jax.experimental.pallas import tpu as pltpu
from jax.sharding import PartitionSpec as P

AXES = ("prow", "pcol")


def ring_order(size):
    return list(range(0, size, 2)) + [i for i in range(size - 1, 0, -1) if i % 2]


def ring_pairs(size):
    order = ring_order(size)
    pairs = []
    for place, row in enumerate(order):
        pairs.append((row * 2, order[(place + 1) % size] * 2))
        pairs.append((row * 2 + 1, order[(place - 1) % size] * 2 + 1))
    return pairs


def accumulate_kernel(count, tail, idx, structure, block_slot, own_inv, other_inv, *refs):
    panels = refs[:count]
    acc, own_panel, tail_tiles, tiles, pcat, tile_sem, panel_sem, tail_sem = refs[count:]
    supers, size = pcat.shape[0], pcat.shape[2]
    rows, cols = own_inv.shape[0], own_inv.shape[1]
    per = panels[0].shape[1]
    me_col = idx[1]

    def copy_tiles(slot, dst, sem):
        mine = slot // cols == me_col
        at = lax.rem(slot, cols)
        for r in range(rows):
            @pl.when(mine)
            def _():
                pltpu.make_async_copy(own_inv.at[r, at], dst(r), sem).start()

            @pl.when(jnp.logical_not(mine))
            def _():
                pltpu.make_async_copy(other_inv.at[r, at], dst(r), sem).start()

    for j in range(count):
        for s in range(supers):
            for k in range(per):
                pltpu.make_async_copy(panels[j].at[s, k], pcat.at[s, j * per + k], panel_sem.at[j]).start()
                slot = block_slot[structure[s, idx[2 + j] * per + k]]
                copy_tiles(slot, lambda r: tiles.at[s, j * per + k, pl.ds(r * size, size)], tile_sem.at[j])
    for j in range(tail):
        for s in range(supers):
            for k in range(per):
                slot = block_slot[structure[s, idx[2 + count + j] * per + k]]
                copy_tiles(slot, lambda r: tail_tiles.at[s, j * per + k, pl.ds(r * size, size)], tail_sem)
    for j in range(count):
        here = pl.ds(j * per, per)
        pltpu.make_async_copy(tiles.at[:, here], tiles.at[:, here], tile_sem.at[j]).wait()
        pltpu.make_async_copy(pcat.at[:, here], pcat.at[:, here], panel_sem.at[j]).wait()
        for s in range(supers):
            for k in range(per):
                part = jnp.dot(tiles[s, j * per + k], pcat[s, j * per + k], preferred_element_type=jnp.float32)
                if j == 0 and k == 0:
                    acc[s] = part
                else:
                    acc[s] += part
    for s in range(supers):
        for r in range(rows):
            row = idx[0] * rows + r
            where = jnp.int32(0)
            found = jnp.int32(0)
            for j in range(count):
                for k in range(per):
                    hit = (block_slot[structure[s, idx[2 + j] * per + k]] == row).astype(jnp.int32)
                    where = where + hit * (j * per + k)
                    found = found + hit
            own_panel[s, pl.ds(r * size, size)] = jnp.where(
                found > 0, pcat[s, where], jnp.zeros((), own_panel.dtype)
            )
    pltpu.make_async_copy(tail_tiles, tail_tiles, tail_sem).wait()


def finish_kernel(count, tail, idx, structure, block_slot, acc, own_panel, tail_tiles, diag, *refs):
    panels = refs[:tail]
    sigma, value = refs[tail:]
    supers, size = acc.shape[0], acc.shape[2]
    rows = acc.shape[1] // size
    per = panels[0].shape[1]
    first = (idx[0] == 0).astype(jnp.float32)
    for s in range(supers):
        total = acc[s]
        for j in range(tail):
            for k in range(per):
                total = total + jnp.dot(
                    tail_tiles[s, j * per + k], panels[j][s, k], preferred_element_type=jnp.float32
                )
        result = diag[pl.ds(s, 1)] * first
        for r in range(rows):
            row = idx[0] * rows + r
            used = jnp.bool_(False)
            for b in range(structure.shape[1]):
                used = jnp.logical_or(used, block_slot[structure[s, b]] == row)
            one = jnp.where(used, -total[r * size:(r + 1) * size], 0.0)
            panel = own_panel[s, pl.ds(r * size, size)].astype(jnp.float32)
            for j in range(tail):
                for k in range(per):
                    hit = block_slot[structure[s, idx[2 + count + j] * per + k]] == row
                    panel = jnp.where(hit, panels[j][s, k].astype(jnp.float32), panel)
            result = result - jnp.sum(panel * one, axis=0, keepdims=True)
            sigma[s, r] = one.astype(sigma.dtype)
        value[pl.ds(s, 1)] = result


def per_device(grid_rows, inverse_tiles, panel_blocks, diag_inverse, structure, block_slot):
    rows, cols, size = inverse_tiles.shape[0], inverse_tiles.shape[1], inverse_tiles.shape[2]
    supers, per = panel_blocks.shape[0], panel_blocks.shape[1]
    pairs = ring_pairs(grid_rows)
    swap = [(i, i ^ 1) for i in range(2 * grid_rows)]
    hop = lambda x: lax.ppermute(x, AXES, pairs)
    cross = lambda x: lax.ppermute(x, AXES, swap)

    mine = hop(panel_blocks)
    theirs_now = cross(panel_blocks)
    other_inverse = cross(inverse_tiles)
    along, across = [mine], []
    for step in range(1, grid_rows // 2 + 1):
        if step <= (grid_rows - 1) // 2:
            theirs_now = hop(theirs_now)
        if step < grid_rows // 2:
            mine = hop(mine)
            along.append(mine)
        if step <= (grid_rows - 1) // 2:
            across.append(cross(theirs_now))

    prow, pcol = lax.axis_index("prow"), lax.axis_index("pcol")
    order = jnp.array(ring_order(grid_rows), jnp.int32)
    half = (grid_rows + 1) // 2
    place = jnp.where(prow % 2 == 0, prow // 2, grid_rows - 1 - prow // 2)
    sign = jnp.where(pcol == 0, -1, 1)

    def row_at(offset):
        at = lax.rem(place + offset + grid_rows, grid_rows)
        return jnp.where(at < half, 2 * at, 2 * (grid_rows - 1 - at) + 1)

    shards = [(panel_blocks, prow)]
    for k in range(1, grid_rows // 2 + 1):
        shards.append((along[k - 1], row_at(sign * k)))
        if k <= (grid_rows - 1) // 2:
            shards.append((across[k - 1], row_at(-sign * k)))
    tail = 2
    count = len(shards) - tail
    idx = jnp.stack([prow, pcol] + [i for _, i in shards]).astype(jnp.int32)

    smem = pl.BlockSpec(memory_space=pltpu.SMEM)
    vmem = pl.BlockSpec(memory_space=pltpu.VMEM)
    hbm = pl.BlockSpec(memory_space=pl.ANY)
    tile = size * size
    acc, own_panel, tail_tiles = pl.pallas_call(
        functools.partial(accumulate_kernel, count, tail),
        out_shape=(
            jax.ShapeDtypeStruct((supers, rows * size, size), jnp.float32),
            jax.ShapeDtypeStruct((supers, rows * size, size), jnp.bfloat16),
            jax.ShapeDtypeStruct((supers, tail * per, rows * size, size), jnp.bfloat16),
        ),
        in_specs=[smem] * 3 + [hbm] * (2 + count),
        out_specs=(vmem, vmem, vmem),
        scratch_shapes=[
            pltpu.VMEM((supers, count * per, rows * size, size), jnp.bfloat16),
            pltpu.VMEM((supers, count * per, size, size), jnp.bfloat16),
            pltpu.SemaphoreType.DMA((count,)),
            pltpu.SemaphoreType.DMA((count,)),
            pltpu.SemaphoreType.DMA,
        ],
        cost_estimate=pl.CostEstimate(
            flops=2 * supers * count * per * rows * tile * size,
            bytes_accessed=2 * supers * (count + tail) * per * (rows + 1) * tile,
            transcendentals=0,
        ),
        name="accumulate",
    )(idx, structure, block_slot, inverse_tiles, other_inverse, *[x for x, _ in shards[:count]])

    sigma, value = pl.pallas_call(
        functools.partial(finish_kernel, count, tail),
        out_shape=(
            jax.ShapeDtypeStruct((supers, rows, size, size), jnp.bfloat16),
            jax.ShapeDtypeStruct(diag_inverse.shape, jnp.float32),
        ),
        in_specs=[smem] * 3 + [vmem] * (4 + tail),
        out_specs=(vmem, vmem),
        cost_estimate=pl.CostEstimate(
            flops=2 * supers * tail * per * rows * tile * size,
            bytes_accessed=supers * rows * tile * 8,
            transcendentals=0,
        ),
        name="finish",
    )(idx, structure, block_slot, acc, own_panel, tail_tiles, diag_inverse, *[x for x, _ in shards[count:]])

    stride = 1
    while stride < grid_rows:
        value = value + lax.ppermute(value, "prow", [(i, i ^ stride) for i in range(grid_rows)])
        stride *= 2
    return sigma, value


def solution(mesh):
    in_specs = (
        P(("fields", "prow"), "pcol", None, None),
        P("fields", "prow", None, "pcol"),
        P("fields", "pcol"),
        P("fields", None),
        P("fields"),
    )
    out_specs = (P("fields", "prow", None, "pcol"), P("fields", "pcol"))
    return jax.shard_map(
        functools.partial(per_device, mesh.shape["prow"]),
        mesh=mesh,
        in_specs=in_specs,
        out_specs=out_specs,
        check_vma=False,
    )
```

time: 96.1 us -> 51.2 us (0.53)
  waiting for transfers between devices: 43.3 us -> 13.1 us
  starting transfers between devices: 0.6 us -> 24.5 us
  blocking collectives: 19 us -> 0 us
  between operations: 14.1 us -> 0.72 us
  Pallas kernels: 0 us -> 8.69 us
  matrix products: 7.51 us -> 0 us
  other arithmetic: 5.67 us -> 1.27 us
  local copies, waits for them, and re-layouts: 5.78 us -> 2.74 us
    all_gather x1 -> x0, waiting for transfers between devices: 40.4 us -> none  [per_device(): lax.all_gather(panel_blocks, 'prow', axis=1, tiled=True)]
    ppermute x1 -> x15, starting transfers between devices: 0.56 us -> 24.5 us  [the longest x7 16.3 us: per_device(): hop = lambda x: lax.ppermute(x, AXES, pairs)]
    psum x1 -> x0, blocking collectives: 19 us -> none  [per_device(): correction = lax.psum(partial_value, 'prow')]
    ppermute x1 -> x15, waiting for transfers between devices: 2.26 us -> 13.1 us  [the longest x7 6.86 us: per_device(): hop = lambda x: lax.ppermute(x, AXES, pairs)]
    pallas_call x0 -> x2, Pallas kernels: none -> 8.69 us  [the longest x1 5.44 us: per_device(): pl.pallas_call(functools.partial(accumulate_kernel, count, tail), out_sha...]
    dot_general x2 -> x0, matrix products: 7.51 us -> none  [the longest x1 4.32 us: make_accumulate(): jnp.einsum('iskxy,skyw->sixw', selected, piece, preferred_element_type=jn...]
    gather x3 -> x0, local copies, waits for them, and re-layouts: 5.68 us -> none  [the longest x1 4.94 us: per_device(): selected = jnp.take(whole_rows, slot_of.reshape(-1), axis=1)]
    select_n x3 -> x0, other arithmetic: 2.55 us -> none  [the longest x1 1.87 us: per_device(): first_half = jnp.where(pcol_index == 0, inverse_tiles, partner)]
  transfers between devices with their start and end apart: 2 -> 15, of which waited for: 2 -> 10; matrix products, arithmetic and copies ran while one was open for 11% -> 1% of each run, Pallas kernels for 0% -> 11%
where the time goes in v1:
time: 51.2 us; the launch traced here: 51 us
  starting transfers between devices  24.5 us (48%)
  waiting for transfers between devices  13.1 us (26%)
  Pallas kernels  8.69 us (17%)
  local copies, waits for them, and re-layouts  2.74 us (5%)
  other arithmetic  1.27 us (2%)
  between operations  0.72 us (1%)
    ppermute x7, starting transfers between devices, per_device(): hop = lambda x: lax.ppermute(x, AXES, pairs)  16.3 us
    ppermute x3, starting transfers between devices, per_device(): lax.ppermute(value, 'prow', [(i, i ^ stride) for i in range(grid_rows)])  7.07 us
    ppermute x7, waiting for transfers between devices, per_device(): hop = lambda x: lax.ppermute(x, AXES, pairs)  6.86 us
    pallas_call x1, Pallas kernels, per_device(): pl.pallas_call(functools.partial(accumulate_kernel, count, tail), out_sha...  5.44 us
    ppermute x3, waiting for transfers between devices, per_device(): lax.ppermute(value, 'prow', [(i, i ^ stride) for i in range(grid_rows)])  4.92 us
    pallas_call x1, Pallas kernels, per_device(): pl.pallas_call(functools.partial(finish_kernel, count, tail), out_shape=(...  3.25 us
    unnamed x12, local copies, waits for them, and re-layouts  2.11 us
    ppermute x5, waiting for transfers between devices, per_device(): cross = lambda x: lax.ppermute(x, AXES, swap)  1.31 us
  transfers between devices with their start and end apart: 15, of which 10 were waited for; matrix products, arithmetic and copies ran while one was open for 1% of the time, Pallas kernels for 11%

profile of v1, /device:TPU:0, one launch (start us, length us, event | category | flops | bytes accessed | tf_op | source)
XLA Modules:
  0.0 51.0 jit_solution(17585312655864028678)
XLA Ops:
  0.6 0.6 %collective-permute-start = (bf16[2,8,256,256]{3,2,1,0:T(8,128)(2,1)}, bf16[2,8,256,256]{3,2,1,0:T(8,128)(2,1)S(1)}, u32[]{:S(2)}, u32[]{:S(2)}) collective-permute-start(bf16[2,8,256,256]{3,2,1,0:T(8,128)(2,1)} %own_inv.1), channel_id=1, source_target_pairs={{0,1},{1,0},{2,3},{3,2},{4,5},{5,4},{6,7},{7,6},{8,9},{9,8},{10,11... | collective-permute-start | bytes 6291464 | tf_op jit(solution)/shard_map/ppermute | solution.py:120
  1.2 0.1 collective-permute-start.2
  1.3 3.0 %collective-permute-start.1 = (bf16[2,1,256,256]{3,2,1,0:T(8,128)(2,1)}, bf16[2,1,256,256]{3,2,1,0:T(8,128)(2,1)S(1)}, u32[]{:S(2)}, u32[]{:S(2)}) collective-permute-start(bf16[2,1,256,256]{3,2,1,0:T(8,128)(2,1)} %refs_0_.1), channel_id=1, source_target_pairs={{0,4},{1,3},{4,8},{5,1},{8,12},{9,5},{12,14},{13,9},{14,10},{15,13... | collective-permute-start | bytes 786440 | tf_op jit(solution)/shard_map/ppermute | solution.py:119
  4.3 1.3 %collective-permute-done.2 = bf16[2,1,256,256]{3,2,1,0:T(8,128)(2,1)S(1)} collective-permute-done((bf16[2,1,256,256]{3,2,1,0:T(8,128)(2,1)}, bf16[2,1,256,256]{3,2,1,0:T(8,128)(2,1)S(1)}, u32[]{:S(2)}, u32[]{:S(2)}) %collective-permute-start.2) | collective-permute-done | bytes 262176 | tf_op jit(solution)/shard_map/ppermute | solution.py:120
  5.6 2.9 %collective-permute-start.3 = (bf16[2,1,256,256]{3,2,1,0:T(8,128)(2,1)S(1)}, bf16[2,1,256,256]{3,2,1,0:T(8,128)(2,1)}, u32[]{:S(2)}, u32[]{:S(2)}) collective-permute-start(bf16[2,1,256,256]{3,2,1,0:T(8,128)(2,1)S(1)} %collective-permute-done.2), channel_id=1, source_target_pairs={{0,4},{1,3},{4,8},{5,1},{8,12},{9,5},{12,14},{13,9},{14,10},{15,13... | collective-permute-start | bytes 786440 | tf_op jit(solution)/shard_map/ppermute | solution.py:119
  8.5 0.3 collective-permute-done.1.refs_1_
  8.8 0.0 copy-start.3
  8.8 2.1 %collective-permute-start.5 = (bf16[2,1,256,256]{3,2,1,0:T(8,128)(2,1)S(1)}, bf16[2,1,256,256]{3,2,1,0:T(8,128)(2,1)S(1)}, u32[]{:S(2)}, u32[]{:S(2)}) collective-permute-start(bf16[2,1,256,256]{3,2,1,0:T(8,128)(2,1)S(1)} %collective-permute-done.1.refs_1_), channel_id=1, source_target_pairs={{0,4},{1,3},{4,8},{5,1},{8,12},{9,5},{12,14},{13,9},{14,10},{15,13... | collective-permute-start | bytes 786440 | tf_op jit(solution)/shard_map/ppermute | solution.py:119
  10.8 2.0 %collective-permute-done.3 = bf16[2,1,256,256]{3,2,1,0:T(8,128)(2,1)} collective-permute-done((bf16[2,1,256,256]{3,2,1,0:T(8,128)(2,1)S(1)}, bf16[2,1,256,256]{3,2,1,0:T(8,128)(2,1)}, u32[]{:S(2)}, u32[]{:S(2)}) %collective-permute-start.3) | collective-permute-done | bytes 262176 | tf_op jit(solution)/shard_map/ppermute | solution.py:119
  12.9 2.1 %collective-permute-start.6 = (bf16[2,1,256,256]{3,2,1,0:T(8,128)(2,1)}, bf16[2,1,256,256]{3,2,1,0:T(8,128)(2,1)}, u32[]{:S(2)}, u32[]{:S(2)}) collective-permute-start(bf16[2,1,256,256]{3,2,1,0:T(8,128)(2,1)} %collective-permute-done.3), channel_id=1, source_target_pairs={{0,4},{1,3},{4,8},{5,1},{8,12},{9,5},{12,14},{13,9},{14,10},{15,13... | collective-permute-start | bytes 786440 | tf_op jit(solution)/shard_map/ppermute | solution.py:119
  15.0 0.6 %collective-permute-done.5.refs_3_ = bf16[2,1,256,256]{3,2,1,0:T(8,128)(2,1)S(1)} collective-permute-done((bf16[2,1,256,256]{3,2,1,0:T(8,128)(2,1)S(1)}, bf16[2,1,256,256]{3,2,1,0:T(8,128)(2,1)S(1)}, u32[]{:S(2)}, u32[]{:S(2)}) %collective-permute-start.5) | collective-permute-done | bytes 262176 | tf_op jit(solution)/shard_map/ppermute | solution.py:119
  15.6 0.0 copy-start.4
  15.6 2.1 %collective-permute-start.8 = (bf16[2,1,256,256]{3,2,1,0:T(8,128)(2,1)S(1)}, bf16[2,1,256,256]{3,2,1,0:T(8,128)(2,1)S(1)}, u32[]{:S(2)}, u32[]{:S(2)}) collective-permute-start(bf16[2,1,256,256]{3,2,1,0:T(8,128)(2,1)S(1)} %collective-permute-done.5.refs_3_), channel_id=1, source_target_pairs={{0,4},{1,3},{4,8},{5,1},{8,12},{9,5},{12,14},{13,9},{14,10},{15,13... | collective-permute-start | bytes 786440 | tf_op jit(solution)/shard_map/ppermute | solution.py:119
  17.7 1.9 %collective-permute-done.6 = bf16[2,1,256,256]{3,2,1,0:T(8,128)(2,1)} collective-permute-done((bf16[2,1,256,256]{3,2,1,0:T(8,128)(2,1)}, bf16[2,1,256,256]{3,2,1,0:T(8,128)(2,1)}, u32[]{:S(2)}, u32[]{:S(2)}) %collective-permute-start.6) | collective-permute-done | bytes 262176 | tf_op jit(solution)/shard_map/ppermute | solution.py:119
  19.6 2.1 %collective-permute-start.9 = (bf16[2,1,256,256]{3,2,1,0:T(8,128)(2,1)}, bf16[2,1,256,256]{3,2,1,0:T(8,128)(2,1)}, u32[]{:S(2)}, u32[]{:S(2)}) collective-permute-start(bf16[2,1,256,256]{3,2,1,0:T(8,128)(2,1)} %collective-permute-done.6), channel_id=1, source_target_pairs={{0,4},{1,3},{4,8},{5,1},{8,12},{9,5},{12,14},{13,9},{14,10},{15,13... | collective-permute-start | bytes 786440 | tf_op jit(solution)/shard_map/ppermute | solution.py:119
  21.7 0.0 collective-permute-start.4
  21.7 0.5 collective-permute-start.7
  22.2 0.1 collective-permute-done.8.refs_5_
  22.3 0.0 copy-start.5
  22.3 2.1 %collective-permute-start.11 = (bf16[2,1,256,256]{3,2,1,0:T(8,128)(2,1)S(1)}, bf16[2,1,256,256]{3,2,1,0:T(8,128)(2,1)S(1)}, u32[]{:S(2)}, u32[]{:S(2)}) collective-permute-start(bf16[2,1,256,256]{3,2,1,0:T(8,128)(2,1)S(1)} %collective-permute-done.8.refs_5_), channel_id=1, source_target_pairs={{0,4},{1,3},{4,8},{5,1},{8,12},{9,5},{12,14},{13,9},{14,10},{15,13... | collective-permute-start | bytes 786440 | tf_op jit(solution)/shard_map/ppermute | solution.py:119
  24.4 1.9 %collective-permute-done.9 = bf16[2,1,256,256]{3,2,1,0:T(8,128)(2,1)} collective-permute-done((bf16[2,1,256,256]{3,2,1,0:T(8,128)(2,1)}, bf16[2,1,256,256]{3,2,1,0:T(8,128)(2,1)}, u32[]{:S(2)}, u32[]{:S(2)}) %collective-permute-start.9) | collective-permute-done | bytes 262176 | tf_op jit(solution)/shard_map/ppermute | solution.py:119
  26.3 0.0 collective-permute-start.10
  26.3 0.6 %stack.40.idx = s32[10]{0:T(128)} concatenate(s32[1]{0:T(128)} %bitcast, s32[1]{0:T(128)} %bitcast.1, s32[1]{0:T(128)} %bitcast, s32[1]{0:T(128)} %bitcast.2, s32[1]{0:T(128)} %bitcast.3, s32[1]{0:T(128)} %bitcast.4, s32[1]{0:T(128)} %bitcast.5, s32[1]{0:T(128)} %bitcast.6, s32[1]{0:T(128)} %bitcast.7, s32[1]{0:T(128)} %bitcast.8), dimensions={0} | concatenate | bytes 80 | tf_op jit(solution)/shard_map/stack | solution.py:152
  26.9 0.0 collective-permute-done.4.refs_2_
  26.9 0.0 collective-permute-done.7.refs_4_
  26.9 0.0 collective-permute-done.other_inv
  26.9 0.0 copy-done.3
  26.9 0.0 copy-done.4
  26.9 0.0 copy-done.5
  26.9 0.0 copy-start
  27.0 1.3 %copy-done = bf16[2,8,256,256]{3,2,1,0:T(8,128)(2,1)} copy-done((bf16[2,8,256,256]{3,2,1,0:T(8,128)(2,1)}, bf16[2,8,256,256]{3,2,1,0:T(8,128)(2,1)S(1)}, u32[]{:S(2)}) %copy-start) | copy-done | bytes 2097176
  28.3 5.4 %accumulate.1 = (f32[2,512,256]{2,1,0:T(8,128)}, bf16[2,512,256]{2,1,0:T(8,128)(2,1)}, bf16[2,2,512,256]{3,2,1,0:T(8,128)(2,1)}) custom-call(s32[10]{0:T(128)} %stack.40.idx, s32[2,8]{1,0:T(2,128)} %structure.3, s32[16]{0:T(128)} %block_slot.3, bf16[2,8,256,256]{3,2,1,0:T(8,128)(2,1)} %own_inv.1, bf16[2,8,256,256]{3,2,1,0:T(8,128)(2,1)} %copy-done, ...), custom_call_target="tpu_custom_call" | custom-call | flops 805306368 | bytes 6291456 | tf_op jit(solution)/shard_map/accumulate/pallas_call | solution.py:158
  33.7 0.0 collective-permute-done.11.refs_1_
  33.7 0.0 copy-start.1
  33.7 0.0 collective-permute-done.10.refs_0_
  33.7 0.0 copy-start.2
  33.8 0.7 %copy-done.1 = bf16[2,1,256,256]{3,2,1,0:T(8,128)(2,1)} copy-done((bf16[2,1,256,256]{3,2,1,0:T(8,128)(2,1)}, bf16[2,1,256,256]{3,2,1,0:T(8,128)(2,1)S(1)}, u32[]{:S(2)}) %copy-start.1) | copy-done | bytes 262168
  34.4 0.1 copy-done.2
  34.5 3.2 %finish.1 = (bf16[2,2,256,256]{3,2,1,0:T(8,128)(2,1)}, f32[2,256]{1,0:T(2,128)}) custom-call(s32[10]{0:T(128)} %stack.40.idx, s32[2,8]{1,0:T(2,128)} %structure.3, s32[16]{0:T(128)} %block_slot.3, f32[2,512,256]{2,1,0:T(8,128)} %get-tuple-element.7.acc, bf16[2,512,256]{2,1,0:T(8,128)(2,1)} %get-tuple-element.8.own_panel, ...), custom_call_target="tpu_custom_call" | custom-call | flops 268435456 | bytes 2097152 | tf_op jit(solution)/shard_map/finish/pallas_call | solution.py:182
  37.8 2.0 %collective-permute-start.12 = (f32[2,256]{1,0:T(2,128)}, f32[2,256]{1,0:T(2,128)S(1)}, u32[]{:S(2)}, u32[]{:S(2)}) collective-permute-start(f32[2,256]{1,0:T(2,128)} %get-tuple-element.11), channel_id=1, source_target_pairs={{0,2},{2,0},{4,6},{6,4},{8,10},{10,8},{12,14},{14,12},{1,3},{3,1},... | collective-permute-start | bytes 6152 | tf_op jit(solution)/shard_map/ppermute | solution.py:200
  39.8 1.8 %collective-permute-done.12 = f32[2,256]{1,0:T(2,128)S(1)} collective-permute-done((f32[2,256]{1,0:T(2,128)}, f32[2,256]{1,0:T(2,128)S(1)}, u32[]{:S(2)}, u32[]{:S(2)}) %collective-permute-start.12) | collective-permute-done | bytes 2080 | tf_op jit(solution)/shard_map/ppermute | solution.py:200
  41.6 0.7 %add.99 = f32[2,256]{1,0:T(2,128)S(1)} add(f32[2,256]{1,0:T(2,128)} %get-tuple-element.11, f32[2,256]{1,0:T(2,128)S(1)} %collective-permute-done.12) | non-fusion elementwise | flops 512 | bytes 6144 | tf_op jit(solution)/shard_map/add | solution.py:200
  42.3 2.0 %collective-permute-start.13 = (f32[2,256]{1,0:T(2,128)S(1)}, f32[2,256]{1,0:T(2,128)S(1)}, u32[]{:S(2)}, u32[]{:S(2)}) collective-permute-start(f32[2,256]{1,0:T(2,128)S(1)} %add.99), channel_id=1, source_target_pairs={{0,4},{2,6},{4,0},{6,2},{8,12},{10,14},{12,8},{14,10},{1,5},{3,7},... | collective-permute-start | bytes 6152 | tf_op jit(solution)/shard_map/ppermute | solution.py:200
  44.3 1.6 %collective-permute-done.13 = f32[2,256]{1,0:T(2,128)S(1)} collective-permute-done((f32[2,256]{1,0:T(2,128)S(1)}, f32[2,256]{1,0:T(2,128)S(1)}, u32[]{:S(2)}, u32[]{:S(2)}) %collective-permute-start.13) | collective-permute-done | bytes 2080 | tf_op jit(solution)/shard_map/ppermute | solution.py:200
  45.9 3.0 %collective-permute-start.14 = (f32[2,256]{1,0:T(2,128)S(1)}, f32[2,256]{1,0:T(2,128)S(1)}, u32[]{:S(2)}, u32[]{:S(2)}) collective-permute-start(f32[2,256]{1,0:T(2,128)S(1)} %add.100), channel_id=1, source_target_pairs={{0,8},{2,10},{4,12},{6,14},{8,0},{10,2},{12,4},{14,6},{1,9},{3,11}... | collective-permute-start | bytes 6152 | tf_op jit(solution)/shard_map/ppermute | solution.py:200
  48.9 1.6 %collective-permute-done.14 = f32[2,256]{1,0:T(2,128)S(1)} collective-permute-done((f32[2,256]{1,0:T(2,128)S(1)}, f32[2,256]{1,0:T(2,128)S(1)}, u32[]{:S(2)}, u32[]{:S(2)}) %collective-permute-start.14) | collective-permute-done | bytes 2080 | tf_op jit(solution)/shard_map/ppermute | solution.py:200
  50.5 0.6 %add.101 = f32[2,256]{1,0:T(2,128)} add(f32[2,256]{1,0:T(2,128)S(1)} %add.100, f32[2,256]{1,0:T(2,128)S(1)} %collective-permute-done.14) | non-fusion elementwise | flops 512 | bytes 6144 | tf_op jit(solution)/shard_map/add | solution.py:200
  (1 shorter events, 0.0 us)
Async XLA Ops:
  0.6 26.3 %collective-permute-start = (bf16[2,8,256,256]{3,2,1,0:T(8,128)(2,1)}, bf16[2,8,256,256]{3,2,1,0:T(8,128)(2,1)S(1)}, u32[]{:S(2)}, u32[]{:S(2)}) collective-permute-start(bf16[2,8,256,256]{3,2,1,0:T(8,128)(2,1)} %own_inv.1), channel_id=1, source_target_pairs={{0,1},{1,0},{2,3},{3,2},{4,5},{5,4},{6,7},{7,6},{8,9},{9,8},{10,11... | collective-permute-start | bytes 6291464 | tf_op jit(solution)/shard_map/ppermute | solution.py:120
  1.2 4.4 %collective-permute-start.2 = (bf16[2,1,256,256]{3,2,1,0:T(8,128)(2,1)}, bf16[2,1,256,256]{3,2,1,0:T(8,128)(2,1)S(1)}, u32[]{:S(2)}, u32[]{:S(2)}) collective-permute-start(bf16[2,1,256,256]{3,2,1,0:T(8,128)(2,1)} %refs_0_.1), channel_id=1, source_target_pairs={{0,1},{1,0},{2,3},{3,2},{4,5},{5,4},{6,7},{7,6},{8,9},{9,8},{10,11... | collective-permute-start | bytes 786440 | tf_op jit(solution)/shard_map/ppermute | solution.py:120
  1.3 7.5 %collective-permute-start.1 = (bf16[2,1,256,256]{3,2,1,0:T(8,128)(2,1)}, bf16[2,1,256,256]{3,2,1,0:T(8,128)(2,1)S(1)}, u32[]{:S(2)}, u32[]{:S(2)}) collective-permute-start(bf16[2,1,256,256]{3,2,1,0:T(8,128)(2,1)} %refs_0_.1), channel_id=1, source_target_pairs={{0,4},{1,3},{4,8},{5,1},{8,12},{9,5},{12,14},{13,9},{14,10},{15,13... | collective-permute-start | bytes 786440 | tf_op jit(solution)/shard_map/ppermute | solution.py:119
  5.6 7.3 %collective-permute-start.3 = (bf16[2,1,256,256]{3,2,1,0:T(8,128)(2,1)S(1)}, bf16[2,1,256,256]{3,2,1,0:T(8,128)(2,1)}, u32[]{:S(2)}, u32[]{:S(2)}) collective-permute-start(bf16[2,1,256,256]{3,2,1,0:T(8,128)(2,1)S(1)} %collective-permute-done.2), channel_id=1, source_target_pairs={{0,4},{1,3},{4,8},{5,1},{8,12},{9,5},{12,14},{13,9},{14,10},{15,13... | collective-permute-start | bytes 786440 | tf_op jit(solution)/shard_map/ppermute | solution.py:119
  8.8 18.2 %copy-start.3 = (bf16[2,1,256,256]{3,2,1,0:T(8,128)(2,1)}, bf16[2,1,256,256]{3,2,1,0:T(8,128)(2,1)S(1)}, u32[]{:S(2)}) copy-start(bf16[2,1,256,256]{3,2,1,0:T(8,128)(2,1)S(1)} %collective-permute-done.1.refs_1_) | copy-start | bytes 786436
  8.8 6.8 %collective-permute-start.5 = (bf16[2,1,256,256]{3,2,1,0:T(8,128)(2,1)S(1)}, bf16[2,1,256,256]{3,2,1,0:T(8,128)(2,1)S(1)}, u32[]{:S(2)}, u32[]{:S(2)}) collective-permute-start(bf16[2,1,256,256]{3,2,1,0:T(8,128)(2,1)S(1)} %collective-permute-done.1.refs_1_), channel_id=1, source_target_pairs={{0,4},{1,3},{4,8},{5,1},{8,12},{9,5},{12,14},{13,9},{14,10},{15,13... | collective-permute-start | bytes 786440 | tf_op jit(solution)/shard_map/ppermute | solution.py:119
  12.9 6.7 %collective-permute-start.6 = (bf16[2,1,256,256]{3,2,1,0:T(8,128)(2,1)}, bf16[2,1,256,256]{3,2,1,0:T(8,128)(2,1)}, u32[]{:S(2)}, u32[]{:S(2)}) collective-permute-start(bf16[2,1,256,256]{3,2,1,0:T(8,128)(2,1)} %collective-permute-done.3), channel_id=1, source_target_pairs={{0,4},{1,3},{4,8},{5,1},{8,12},{9,5},{12,14},{13,9},{14,10},{15,13... | collective-permute-start | bytes 786440 | tf_op jit(solution)/shard_map/ppermute | solution.py:119
  15.6 11.3 %copy-start.4 = (bf16[2,1,256,256]{3,2,1,0:T(8,128)(2,1)}, bf16[2,1,256,256]{3,2,1,0:T(8,128)(2,1)S(1)}, u32[]{:S(2)}) copy-start(bf16[2,1,256,256]{3,2,1,0:T(8,128)(2,1)S(1)} %collective-permute-done.5.refs_3_) | copy-start | bytes 786436
  15.6 6.7 %collective-permute-start.8 = (bf16[2,1,256,256]{3,2,1,0:T(8,128)(2,1)S(1)}, bf16[2,1,256,256]{3,2,1,0:T(8,128)(2,1)S(1)}, u32[]{:S(2)}, u32[]{:S(2)}) collective-permute-start(bf16[2,1,256,256]{3,2,1,0:T(8,128)(2,1)S(1)} %collective-permute-done.5.refs_3_), channel_id=1, source_target_pairs={{0,4},{1,3},{4,8},{5,1},{8,12},{9,5},{12,14},{13,9},{14,10},{15,13... | collective-permute-start | bytes 786440 | tf_op jit(solution)/shard_map/ppermute | solution.py:119
  19.6 6.7 %collective-permute-start.9 = (bf16[2,1,256,256]{3,2,1,0:T(8,128)(2,1)}, bf16[2,1,256,256]{3,2,1,0:T(8,128)(2,1)}, u32[]{:S(2)}, u32[]{:S(2)}) collective-permute-start(bf16[2,1,256,256]{3,2,1,0:T(8,128)(2,1)} %collective-permute-done.6), channel_id=1, source_target_pairs={{0,4},{1,3},{4,8},{5,1},{8,12},{9,5},{12,14},{13,9},{14,10},{15,13... | collective-permute-start | bytes 786440 | tf_op jit(solution)/shard_map/ppermute | solution.py:119
  21.7 5.2 %collective-permute-start.4 = (bf16[2,1,256,256]{3,2,1,0:T(8,128)(2,1)}, bf16[2,1,256,256]{3,2,1,0:T(8,128)(2,1)}, u32[]{:S(2)}, u32[]{:S(2)}) collective-permute-start(bf16[2,1,256,256]{3,2,1,0:T(8,128)(2,1)} %collective-permute-done.3), channel_id=1, source_target_pairs={{0,1},{1,0},{2,3},{3,2},{4,5},{5,4},{6,7},{7,6},{8,9},{9,8},{10,11... | collective-permute-start | bytes 786440 | tf_op jit(solution)/shard_map/ppermute | solution.py:120
  21.7 5.2 %collective-permute-start.7 = (bf16[2,1,256,256]{3,2,1,0:T(8,128)(2,1)}, bf16[2,1,256,256]{3,2,1,0:T(8,128)(2,1)}, u32[]{:S(2)}, u32[]{:S(2)}) collective-permute-start(bf16[2,1,256,256]{3,2,1,0:T(8,128)(2,1)} %collective-permute-done.6), channel_id=1, source_target_pairs={{0,1},{1,0},{2,3},{3,2},{4,5},{5,4},{6,7},{7,6},{8,9},{9,8},{10,11... | collective-permute-start | bytes 786440 | tf_op jit(solution)/shard_map/ppermute | solution.py:120
  22.3 4.7 %copy-start.5 = (bf16[2,1,256,256]{3,2,1,0:T(8,128)(2,1)}, bf16[2,1,256,256]{3,2,1,0:T(8,128)(2,1)S(1)}, u32[]{:S(2)}) copy-start(bf16[2,1,256,256]{3,2,1,0:T(8,128)(2,1)S(1)} %collective-permute-done.8.refs_5_) | copy-start | bytes 786436
  22.3 11.4 %collective-permute-start.11 = (bf16[2,1,256,256]{3,2,1,0:T(8,128)(2,1)S(1)}, bf16[2,1,256,256]{3,2,1,0:T(8,128)(2,1)S(1)}, u32[]{:S(2)}, u32[]{:S(2)}) collective-permute-start(bf16[2,1,256,256]{3,2,1,0:T(8,128)(2,1)S(1)} %collective-permute-done.8.refs_5_), channel_id=1, source_target_pairs={{0,4},{1,3},{4,8},{5,1},{8,12},{9,5},{12,14},{13,9},{14,10},{15,13... | collective-permute-start | bytes 786440 | tf_op jit(solution)/shard_map/ppermute | solution.py:119
  26.3 7.5 %collective-permute-start.10 = (bf16[2,1,256,256]{3,2,1,0:T(8,128)(2,1)}, bf16[2,1,256,256]{3,2,1,0:T(8,128)(2,1)S(1)}, u32[]{:S(2)}, u32[]{:S(2)}) collective-permute-start(bf16[2,1,256,256]{3,2,1,0:T(8,128)(2,1)} %collective-permute-done.9), channel_id=1, source_target_pairs={{0,1},{1,0},{2,3},{3,2},{4,5},{5,4},{6,7},{7,6},{8,9},{9,8},{10,11... | collective-permute-start | bytes 786440 | tf_op jit(solution)/shard_map/ppermute | solution.py:120
  26.9 1.3 %copy-start = (bf16[2,8,256,256]{3,2,1,0:T(8,128)(2,1)}, bf16[2,8,256,256]{3,2,1,0:T(8,128)(2,1)S(1)}, u32[]{:S(2)}) copy-start(bf16[2,8,256,256]{3,2,1,0:T(8,128)(2,1)S(1)} %collective-permute-done.other_inv) | copy-start | bytes 6291460
  33.7 0.7 %copy-start.1 = (bf16[2,1,256,256]{3,2,1,0:T(8,128)(2,1)}, bf16[2,1,256,256]{3,2,1,0:T(8,128)(2,1)S(1)}, u32[]{:S(2)}) copy-start(bf16[2,1,256,256]{3,2,1,0:T(8,128)(2,1)S(1)} %collective-permute-done.11.refs_1_) | copy-start | bytes 786436
  33.7 0.8 %copy-start.2 = (bf16[2,1,256,256]{3,2,1,0:T(8,128)(2,1)}, bf16[2,1,256,256]{3,2,1,0:T(8,128)(2,1)S(1)}, u32[]{:S(2)}) copy-start(bf16[2,1,256,256]{3,2,1,0:T(8,128)(2,1)S(1)} %collective-permute-done.10.refs_0_) | copy-start | bytes 786436
  37.8 3.8 %collective-permute-start.12 = (f32[2,256]{1,0:T(2,128)}, f32[2,256]{1,0:T(2,128)S(1)}, u32[]{:S(2)}, u32[]{:S(2)}) collective-permute-start(f32[2,256]{1,0:T(2,128)} %get-tuple-element.11), channel_id=1, source_target_pairs={{0,2},{2,0},{4,6},{6,4},{8,10},{10,8},{12,14},{14,12},{1,3},{3,1},... | collective-permute-start | bytes 6152 | tf_op jit(solution)/shard_map/ppermute | solution.py:200
  42.3 3.6 %collective-permute-start.13 = (f32[2,256]{1,0:T(2,128)S(1)}, f32[2,256]{1,0:T(2,128)S(1)}, u32[]{:S(2)}, u32[]{:S(2)}) collective-permute-start(f32[2,256]{1,0:T(2,128)S(1)} %add.99), channel_id=1, source_target_pairs={{0,4},{2,6},{4,0},{6,2},{8,12},{10,14},{12,8},{14,10},{1,5},{3,7},... | collective-permute-start | bytes 6152 | tf_op jit(solution)/shard_map/ppermute | solution.py:200
  45.9 4.6 %collective-permute-start.14 = (f32[2,256]{1,0:T(2,128)S(1)}, f32[2,256]{1,0:T(2,128)S(1)}, u32[]{:S(2)}, u32[]{:S(2)}) collective-permute-start(f32[2,256]{1,0:T(2,128)S(1)} %add.100), channel_id=1, source_target_pairs={{0,8},{2,10},{4,12},{6,14},{8,0},{10,2},{12,4},{14,6},{1,9},{3,11}... | collective-permute-start | bytes 6152 | tf_op jit(solution)/shard_map/ppermute | solution.py:200

commit v2 on v0

v2 whole, which is shorter than its diff:
```python
import functools
import jax
import jax.numpy as jnp
from jax import lax
from jax.experimental import pallas as pl
from jax.experimental.pallas import tpu as pltpu
from jax.sharding import PartitionSpec as P

AXES = ("prow", "pcol")


def ring_order(size):
    return list(range(0, size, 2)) + [i for i in range(size - 1, 0, -1) if i % 2]


def ring_pairs(size):
    order = ring_order(size)
    pairs = []
    for place, row in enumerate(order):
        pairs.append((row * 2, order[(place + 1) % size] * 2))
        pairs.append((row * 2 + 1, order[(place - 1) % size] * 2 + 1))
    return pairs


class Place:
    def __init__(self, size):
        self.size = size
        self.prow = lax.axis_index("prow")
        self.pcol = lax.axis_index("pcol")
        odd = self.prow & 1
        half = self.prow >> 1
        self.at = half + odd * (size - 1 - 2 * half)

    def row(self, steps):
        if steps == 0:
            return self.prow
        at = lax.rem(self.at + self.size - steps * (1 - 2 * self.pcol), self.size)
        return jnp.where(2 * at < self.size, 2 * at, 2 * (self.size - 1 - at) + 1)


def load_kernel(source, target, sem):
    copy = pltpu.make_async_copy(source, target, sem)
    copy.start()
    copy.wait()


def add_products(place, steps, structure, block_slot, own, other, panels, acc, fresh):
    rows, cols, size = own.shape[0], own.shape[1], own.shape[2]
    for j, panel in enumerate(panels):
        shard_row = place.row(steps[j])
        per = panel.shape[1]
        for s in range(panel.shape[0]):
            for k in range(per):
                slot = block_slot[structure[s, shard_row * per + k]]
                mine = slot // cols == place.pcol
                at = lax.rem(slot, cols)
                for r in range(rows):
                    tile = jnp.where(mine, own[r, at], other[r, at])
                    part = jnp.dot(tile, panel[s, k], preferred_element_type=jnp.float32)
                    here = pl.ds(r * size, size)
                    if fresh and j == 0 and k == 0:
                        acc[s, here] = part
                    else:
                        acc[s, here] += part


def panel_hits(place, steps, structure, block_slot, panels, rows, s, r):
    per = panels[0].shape[1]
    for j, panel in enumerate(panels):
        for k in range(per):
            yield block_slot[structure[s, place.row(steps[j]) * per + k]] == place.prow * rows + r, panel, k


def accumulate_kernel(grid_rows, steps, structure, block_slot, own, other, *refs):
    panels, (acc, own_panel) = refs[:len(steps)], refs[len(steps):]
    place = Place(grid_rows)
    rows, size = own.shape[0], own.shape[2]
    own_panel[...] = jnp.zeros_like(own_panel)
    for s in range(acc.shape[0]):
        for r in range(rows):
            for hit, panel, k in panel_hits(place, steps, structure, block_slot, panels, rows, s, r):
                @pl.when(hit)
                def _():
                    own_panel[s, pl.ds(r * size, size)] = panel[s, k]
    add_products(place, steps, structure, block_slot, own, other, panels, acc, True)


def finish_kernel(grid_rows, steps, structure, block_slot, own, other, acc, own_panel, diag, *refs):
    panels, (sigma, value, total, panel_rows) = refs[:len(steps)], refs[len(steps):]
    place = Place(grid_rows)
    rows, size = own.shape[0], own.shape[2]
    supers = acc.shape[0]
    total[...] = acc[...]
    panel_rows[...] = own_panel[...]
    add_products(place, steps, structure, block_slot, own, other, panels, total, False)
    first = (place.prow == 0).astype(jnp.float32)
    for s in range(supers):
        result = diag[pl.ds(s, 1)] * first
        for r in range(rows):
            here = pl.ds(r * size, size)
            for hit, panel, k in panel_hits(place, steps, structure, block_slot, panels, rows, s, r):
                @pl.when(hit)
                def _():
                    panel_rows[s, here] = panel[s, k]
            used = jnp.bool_(False)
            for b in range(structure.shape[1]):
                used = jnp.logical_or(used, block_slot[structure[s, b]] == place.prow * rows + r)
            one = jnp.where(used, -total[s, here], 0.0)
            result = result - jnp.sum(panel_rows[s, here].astype(jnp.float32) * one, axis=0, keepdims=True)
            sigma[s, r] = one.astype(sigma.dtype)
        value[pl.ds(s, 1)] = result


def per_device(grid_rows, inverse_tiles, panel_blocks, diag_inverse, structure, block_slot):
    rows, size = inverse_tiles.shape[0], inverse_tiles.shape[2]
    supers, per = panel_blocks.shape[0], panel_blocks.shape[1]
    pairs = ring_pairs(grid_rows)
    swap = [(i, i ^ 1) for i in range(2 * grid_rows)]
    ways, backs = grid_rows // 2, (grid_rows - 1) // 2

    def hop(x):
        return lax.ppermute(x, AXES, pairs)

    def cross(x):
        return lax.ppermute(x, AXES, swap)

    smem = pl.BlockSpec(memory_space=pltpu.SMEM)
    vmem = pl.BlockSpec(memory_space=pltpu.VMEM)
    hbm = pl.BlockSpec(memory_space=pltpu.HBM)

    mine = hop(panel_blocks)
    theirs = cross(panel_blocks)
    own = pl.pallas_call(
        load_kernel,
        out_shape=jax.ShapeDtypeStruct(inverse_tiles.shape, inverse_tiles.dtype),
        in_specs=[hbm],
        out_specs=vmem,
        scratch_shapes=[pltpu.SemaphoreType.DMA],
        compiler_params=pltpu.CompilerParams(vmem_limit_bytes=4 << 20),
        name="load",
    )(inverse_tiles)
    other = cross(inverse_tiles)
    shards = [(0, panel_blocks), (1, mine)]
    for step in range(1, ways + 1):
        if step <= backs:
            theirs = hop(theirs)
        if step < ways:
            mine = hop(mine)
        if step <= backs:
            shards.append((-step, cross(theirs)))
        if step < ways:
            shards.append((step + 1, mine))
    tail = min(2, len(shards) - 1)
    count = len(shards) - tail
    early, late = shards[:count], shards[count:]

    tile = size * size
    small = pltpu.CompilerParams(vmem_limit_bytes=8 << 20)
    acc, own_panel = pl.pallas_call(
        functools.partial(accumulate_kernel, grid_rows, [k for k, _ in early]),
        out_shape=(
            jax.ShapeDtypeStruct((supers, rows * size, size), jnp.float32),
            jax.ShapeDtypeStruct((supers, rows * size, size), jnp.bfloat16),
        ),
        in_specs=[smem] * 2 + [vmem] * (2 + count),
        out_specs=(vmem, vmem),
        compiler_params=small,
        cost_estimate=pl.CostEstimate(
            flops=2 * supers * count * per * rows * tile * size,
            bytes_accessed=2 * supers * count * per * (rows + 1) * tile,
            transcendentals=0,
        ),
        name="accumulate",
    )(structure, block_slot, own, other, *[x for _, x in early])

    sigma, value = pl.pallas_call(
        functools.partial(finish_kernel, grid_rows, [k for k, _ in late]),
        out_shape=(
            jax.ShapeDtypeStruct((supers, rows, size, size), jnp.bfloat16),
            jax.ShapeDtypeStruct(diag_inverse.shape, jnp.float32),
        ),
        in_specs=[smem] * 2 + [vmem] * (5 + tail),
        out_specs=(vmem, vmem),
        scratch_shapes=[
            pltpu.VMEM((supers, rows * size, size), jnp.float32),
            pltpu.VMEM((supers, rows * size, size), jnp.bfloat16),
        ],
        compiler_params=small,
        cost_estimate=pl.CostEstimate(
            flops=2 * supers * tail * per * rows * tile * size,
            bytes_accessed=supers * rows * tile * 8,
            transcendentals=0,
        ),
        name="finish",
    )(structure, block_slot, own, other, acc, own_panel, diag_inverse, *[x for _, x in late])

    stride = 1
    while stride < grid_rows:
        value = value + lax.ppermute(value, "prow", [(i, i ^ stride) for i in range(grid_rows)])
        stride *= 2
    return sigma, value


def solution(mesh):
    in_specs = (
        P(("fields", "prow"), "pcol", None, None),
        P("fields", "prow", None, "pcol"),
        P("fields", "pcol"),
        P("fields", None),
        P("fields"),
    )
    out_specs = (P("fields", "prow", None, "pcol"), P("fields", "pcol"))
    grid_rows = mesh.shape["prow"]

    def body(*args):
        return per_device(grid_rows, *args)

    return jax.shard_map(body, mesh=mesh, in_specs=in_specs, out_specs=out_specs, check_vma=False)
```

time: 96.1 us -> 44.7 us (0.47)
  waiting for transfers between devices: 43.3 us -> 12.1 us
  starting transfers between devices: 0.6 us -> 24.6 us
  blocking collectives: 19 us -> 0 us
  between operations: 14.1 us -> 0.72 us
  matrix products: 7.51 us -> 0 us
  other arithmetic: 5.67 us -> 0.59 us
  Pallas kernels: 0 us -> 4.19 us
  local copies, waits for them, and re-layouts: 5.78 us -> 2.35 us
    all_gather x1 -> x0, waiting for transfers between devices: 40.4 us -> none  [per_device(): lax.all_gather(panel_blocks, 'prow', axis=1, tiled=True)]
    ppermute x1 -> x15, starting transfers between devices: 0.56 us -> 24.6 us  [the longest x7 16.3 us: hop(): return lax.ppermute(x, AXES, pairs)]
    psum x1 -> x0, blocking collectives: 19 us -> none  [per_device(): correction = lax.psum(partial_value, 'prow')]
    ppermute x1 -> x15, waiting for transfers between devices: 2.26 us -> 12.1 us  [the longest x7 6.13 us: hop(): return lax.ppermute(x, AXES, pairs)]
    dot_general x2 -> x0, matrix products: 7.51 us -> none  [the longest x1 4.32 us: make_accumulate(): jnp.einsum('iskxy,skyw->sixw', selected, piece, preferred_element_type=jn...]
    gather x3 -> x0, local copies, waits for them, and re-layouts: 5.68 us -> none  [the longest x1 4.94 us: per_device(): selected = jnp.take(whole_rows, slot_of.reshape(-1), axis=1)]
    pallas_call x0 -> x3, Pallas kernels: none -> 4.19 us  [the longest x1 2.14 us: per_device(): pl.pallas_call(functools.partial(finish_kernel, grid_rows, [k for k, _ in...]
    select_n x3 -> x0, other arithmetic: 2.55 us -> none  [the longest x1 1.87 us: per_device(): first_half = jnp.where(pcol_index == 0, inverse_tiles, partner)]
  transfers between devices with their start and end apart: 2 -> 15, of which waited for: 2 -> 10; matrix products, arithmetic and copies ran while one was open for 11% -> 0% of each run, Pallas kernels for 0% -> 5%
where the time goes in v2:
time: 44.7 us; the launch traced here: 44.6 us
  starting transfers between devices  24.6 us (55%)
  waiting for transfers between devices  12.1 us (27%)
  Pallas kernels  4.19 us (9%)
  local copies, waits for them, and re-layouts  2.35 us (5%)
  between operations  0.72 us (2%)
  other arithmetic  0.59 us (1%)
    ppermute x7, starting transfers between devices, hop(): return lax.ppermute(x, AXES, pairs)  16.3 us
    ppermute x3, starting transfers between devices, per_device(): lax.ppermute(value, 'prow', [(i, i ^ stride) for i in range(grid_rows)])  7.12 us
    ppermute x7, waiting for transfers between devices, hop(): return lax.ppermute(x, AXES, pairs)  6.13 us
    ppermute x3, waiting for transfers between devices, per_device(): lax.ppermute(value, 'prow', [(i, i ^ stride) for i in range(grid_rows)])  4.69 us
    unnamed x10, local copies, waits for them, and re-layouts  2.35 us
    pallas_call x1, Pallas kernels, per_device(): pl.pallas_call(functools.partial(finish_kernel, grid_rows, [k for k, _ in...  2.14 us
    pallas_call x1, Pallas kernels, per_device(): pl.pallas_call(functools.partial(accumulate_kernel, grid_rows, [k for k,...  1.9 us
    ppermute x5, waiting for transfers between devices, cross(): return lax.ppermute(x, AXES, swap)  1.31 us
  transfers between devices with their start and end apart: 15, of which 10 were waited for; matrix products, arithmetic and copies ran while one was open for 0% of the time, Pallas kernels for 5%

profile of v2, /device:TPU:0, one launch (start us, length us, event | category | flops | bytes accessed | tf_op | source)
XLA Modules:
  0.0 44.6 jit_solution(15702629724173056585)
XLA Ops:
  0.6 0.6 %collective-permute-start = (bf16[2,8,256,256]{3,2,1,0:T(8,128)(2,1)}, bf16[2,8,256,256]{3,2,1,0:T(8,128)(2,1)S(1)}, u32[]{:S(2)}, u32[]{:S(2)}) collective-permute-start(bf16[2,8,256,256]{3,2,1,0:T(8,128)(2,1)} %source.1), channel_id=1, source_target_pairs={{0,1},{1,0},{2,3},{3,2},{4,5},{5,4},{6,7},{7,6},{8,9},{9,8},{10,11... | collective-permute-start | bytes 6291464 | tf_op jit(solution)/shard_map/ppermute | solution.py:125
  1.2 0.1 collective-permute-start.2
  1.3 3.0 %collective-permute-start.1 = (bf16[2,1,256,256]{3,2,1,0:T(8,128)(2,1)}, bf16[2,1,256,256]{3,2,1,0:T(8,128)(2,1)S(1)}, u32[]{:S(2)}, u32[]{:S(2)}) collective-permute-start(bf16[2,1,256,256]{3,2,1,0:T(8,128)(2,1)} %refs_0_.1), channel_id=1, source_target_pairs={{0,4},{1,3},{4,8},{5,1},{8,12},{9,5},{12,14},{13,9},{14,10},{15,13... | collective-permute-start | bytes 786440 | tf_op jit(solution)/shard_map/ppermute | solution.py:122
  4.3 1.3 %collective-permute-done.2 = bf16[2,1,256,256]{3,2,1,0:T(8,128)(2,1)S(1)} collective-permute-done((bf16[2,1,256,256]{3,2,1,0:T(8,128)(2,1)}, bf16[2,1,256,256]{3,2,1,0:T(8,128)(2,1)S(1)}, u32[]{:S(2)}, u32[]{:S(2)}) %collective-permute-start.2) | collective-permute-done | bytes 262176 | tf_op jit(solution)/shard_map/ppermute | solution.py:125
  5.6 2.9 %collective-permute-start.3 = (bf16[2,1,256,256]{3,2,1,0:T(8,128)(2,1)S(1)}, bf16[2,1,256,256]{3,2,1,0:T(8,128)(2,1)S(1)}, u32[]{:S(2)}, u32[]{:S(2)}) collective-permute-start(bf16[2,1,256,256]{3,2,1,0:T(8,128)(2,1)S(1)} %collective-permute-done.2), channel_id=1, source_target_pairs={{0,4},{1,3},{4,8},{5,1},{8,12},{9,5},{12,14},{13,9},{14,10},{15,13... | collective-permute-start | bytes 786440 | tf_op jit(solution)/shard_map/ppermute | solution.py:122
  8.5 0.3 collective-permute-done.1.refs_1_
  8.8 2.1 %collective-permute-start.5 = (bf16[2,1,256,256]{3,2,1,0:T(8,128)(2,1)S(1)}, bf16[2,1,256,256]{3,2,1,0:T(8,128)(2,1)S(1)}, u32[]{:S(2)}, u32[]{:S(2)}) collective-permute-start(bf16[2,1,256,256]{3,2,1,0:T(8,128)(2,1)S(1)} %collective-permute-done.1.refs_1_), channel_id=1, source_target_pairs={{0,4},{1,3},{4,8},{5,1},{8,12},{9,5},{12,14},{13,9},{14,10},{15,13... | collective-permute-start | bytes 786440 | tf_op jit(solution)/shard_map/ppermute | solution.py:122
  10.8 1.9 %collective-permute-done.3 = bf16[2,1,256,256]{3,2,1,0:T(8,128)(2,1)S(1)} collective-permute-done((bf16[2,1,256,256]{3,2,1,0:T(8,128)(2,1)S(1)}, bf16[2,1,256,256]{3,2,1,0:T(8,128)(2,1)S(1)}, u32[]{:S(2)}, u32[]{:S(2)}) %collective-permute-start.3) | collective-permute-done | bytes 262176 | tf_op jit(solution)/shard_map/ppermute | solution.py:122
  12.8 2.1 %collective-permute-start.6 = (bf16[2,1,256,256]{3,2,1,0:T(8,128)(2,1)S(1)}, bf16[2,1,256,256]{3,2,1,0:T(8,128)(2,1)S(1)}, u32[]{:S(2)}, u32[]{:S(2)}) collective-permute-start(bf16[2,1,256,256]{3,2,1,0:T(8,128)(2,1)S(1)} %collective-permute-done.3), channel_id=1, source_target_pairs={{0,4},{1,3},{4,8},{5,1},{8,12},{9,5},{12,14},{13,9},{14,10},{15,13... | collective-permute-start | bytes 786440 | tf_op jit(solution)/shard_map/ppermute | solution.py:122
  14.9 0.7 %collective-permute-done.5.refs_3_ = bf16[2,1,256,256]{3,2,1,0:T(8,128)(2,1)S(1)} collective-permute-done((bf16[2,1,256,256]{3,2,1,0:T(8,128)(2,1)S(1)}, bf16[2,1,256,256]{3,2,1,0:T(8,128)(2,1)S(1)}, u32[]{:S(2)}, u32[]{:S(2)}) %collective-permute-start.5) | collective-permute-done | bytes 262176 | tf_op jit(solution)/shard_map/ppermute | solution.py:122
  15.6 2.1 %collective-permute-start.8 = (bf16[2,1,256,256]{3,2,1,0:T(8,128)(2,1)S(1)}, bf16[2,1,256,256]{3,2,1,0:T(8,128)(2,1)S(1)}, u32[]{:S(2)}, u32[]{:S(2)}) collective-permute-start(bf16[2,1,256,256]{3,2,1,0:T(8,128)(2,1)S(1)} %collective-permute-done.5.refs_3_), channel_id=1, source_target_pairs={{0,4},{1,3},{4,8},{5,1},{8,12},{9,5},{12,14},{13,9},{14,10},{15,13... | collective-permute-start | bytes 786440 | tf_op jit(solution)/shard_map/ppermute | solution.py:122
  17.7 1.5 %collective-permute-done.6 = bf16[2,1,256,256]{3,2,1,0:T(8,128)(2,1)S(1)} collective-permute-done((bf16[2,1,256,256]{3,2,1,0:T(8,128)(2,1)S(1)}, bf16[2,1,256,256]{3,2,1,0:T(8,128)(2,1)S(1)}, u32[]{:S(2)}, u32[]{:S(2)}) %collective-permute-start.6) | collective-permute-done | bytes 262176 | tf_op jit(solution)/shard_map/ppermute | solution.py:122
  19.2 2.1 %collective-permute-start.9 = (bf16[2,1,256,256]{3,2,1,0:T(8,128)(2,1)S(1)}, bf16[2,1,256,256]{3,2,1,0:T(8,128)(2,1)S(1)}, u32[]{:S(2)}, u32[]{:S(2)}) collective-permute-start(bf16[2,1,256,256]{3,2,1,0:T(8,128)(2,1)S(1)} %collective-permute-done.6), channel_id=1, source_target_pairs={{0,4},{1,3},{4,8},{5,1},{8,12},{9,5},{12,14},{13,9},{14,10},{15,13... | collective-permute-start | bytes 786440 | tf_op jit(solution)/shard_map/ppermute | solution.py:122
  21.2 0.0 collective-permute-start.4
  21.2 0.5 %collective-permute-start.7 = (bf16[2,1,256,256]{3,2,1,0:T(8,128)(2,1)S(1)}, bf16[2,1,256,256]{3,2,1,0:T(8,128)(2,1)S(1)}, u32[]{:S(2)}, u32[]{:S(2)}) collective-permute-start(bf16[2,1,256,256]{3,2,1,0:T(8,128)(2,1)S(1)} %collective-permute-done.6), channel_id=1, source_target_pairs={{0,1},{1,0},{2,3},{3,2},{4,5},{5,4},{6,7},{7,6},{8,9},{9,8},{10,11... | collective-permute-start | bytes 786440 | tf_op jit(solution)/shard_map/ppermute | solution.py:125
  21.8 0.2 collective-permute-done.8.refs_5_
  22.0 2.1 %collective-permute-start.11 = (bf16[2,1,256,256]{3,2,1,0:T(8,128)(2,1)S(1)}, bf16[2,1,256,256]{3,2,1,0:T(8,128)(2,1)S(1)}, u32[]{:S(2)}, u32[]{:S(2)}) collective-permute-start(bf16[2,1,256,256]{3,2,1,0:T(8,128)(2,1)S(1)} %collective-permute-done.8.refs_5_), channel_id=1, source_target_pairs={{0,4},{1,3},{4,8},{5,1},{8,12},{9,5},{12,14},{13,9},{14,10},{15,13... | collective-permute-start | bytes 786440 | tf_op jit(solution)/shard_map/ppermute | solution.py:122
  24.0 1.5 %collective-permute-done.9 = bf16[2,1,256,256]{3,2,1,0:T(8,128)(2,1)S(1)} collective-permute-done((bf16[2,1,256,256]{3,2,1,0:T(8,128)(2,1)S(1)}, bf16[2,1,256,256]{3,2,1,0:T(8,128)(2,1)S(1)}, u32[]{:S(2)}, u32[]{:S(2)}) %collective-permute-start.9) | collective-permute-done | bytes 262176 | tf_op jit(solution)/shard_map/ppermute | solution.py:122
  25.5 0.0 collective-permute-start.10
  25.5 0.0 copy-start
  25.5 1.6 %copy-done = bf16[2,8,256,256]{3,2,1,0:T(8,128)(2,1)S(1)} copy-done((bf16[2,8,256,256]{3,2,1,0:T(8,128)(2,1)S(1)}, bf16[2,8,256,256]{3,2,1,0:T(8,128)(2,1)}, u32[]{:S(2)}) %copy-start) | copy-done | bytes 2097176
  27.1 0.0 copy-start.1
  27.1 0.0 copy-start.2
  27.1 0.0 copy-start.4
  27.1 0.1 load.1.own
  27.3 0.0 copy-start.3
  27.3 0.0 collective-permute-done.4.refs_2_
  27.3 0.0 collective-permute-done.7.refs_4_
  27.3 0.0 collective-permute-done.other
  27.3 0.7 %copy-done.1 = bf16[2,1,256,256]{3,2,1,0:T(8,128)(2,1)S(1)} copy-done((bf16[2,1,256,256]{3,2,1,0:T(8,128)(2,1)S(1)}, bf16[2,1,256,256]{3,2,1,0:T(8,128)(2,1)}, u32[]{:S(2)}) %copy-start.1) | copy-done | bytes 262168
  28.1 0.0 copy-done.2
  28.1 0.0 copy-done.4
  28.1 1.9 %accumulate.1 = (f32[2,512,256]{2,1,0:T(8,128)S(1)}, bf16[2,512,256]{2,1,0:T(8,128)(2,1)S(1)}) custom-call(s32[2,8]{1,0:T(2,128)S(1)} %copy-done.2, s32[16]{0:T(128)S(1)} %copy-done.4, bf16[2,8,256,256]{3,2,1,0:T(8,128)(2,1)S(1)} %load.1.own, bf16[2,8,256,256]{3,2,1,0:T(8,128)(2,1)S(1)} %collective-permute-done.other, ...), custom_call_target="tpu_custom_call" | custom-call | flops 805306368 | bytes 4718592 | tf_op jit(solution)/shard_map/accumulate/pallas_call | solution.py:159
  30.0 0.0 collective-permute-done.11.refs_1_
  30.0 0.0 collective-permute-done.10.refs_0_
  30.0 0.0 copy-done.3
  30.0 2.1 %finish.1 = (bf16[2,2,256,256]{3,2,1,0:T(8,128)(2,1)}, f32[2,256]{1,0:T(2,128)S(1)}) custom-call(s32[2,8]{1,0:T(2,128)S(1)} %copy-done.2, s32[16]{0:T(128)S(1)} %copy-done.4, bf16[2,8,256,256]{3,2,1,0:T(8,128)(2,1)S(1)} %load.1.own, bf16[2,8,256,256]{3,2,1,0:T(8,128)(2,1)S(1)} %collective-permute-done.other, f32[2,512,256]{2,1,0:T(8,128)S(1)} %get-tuple-element.6.acc, ...), custom_call_target="tpu_custom_call" | custom-call | flops 268435456 | bytes 2097152 | tf_op jit(solution)/shard_map/finish/pallas_call | solution.py:176
  32.2 2.0 %collective-permute-start.12 = (f32[2,256]{1,0:T(2,128)S(1)}, f32[2,256]{1,0:T(2,128)S(1)}, u32[]{:S(2)}, u32[]{:S(2)}) collective-permute-start(f32[2,256]{1,0:T(2,128)S(1)} %get-tuple-element.9), channel_id=1, source_target_pairs={{0,2},{2,0},{4,6},{6,4},{8,10},{10,8},{12,14},{14,12},{1,3},{3,1},... | collective-permute-start | bytes 6152 | tf_op jit(solution)/shard_map/ppermute | solution.py:199
  34.2 1.6 %collective-permute-done.12 = f32[2,256]{1,0:T(2,128)S(1)} collective-permute-done((f32[2,256]{1,0:T(2,128)S(1)}, f32[2,256]{1,0:T(2,128)S(1)}, u32[]{:S(2)}, u32[]{:S(2)}) %collective-permute-start.12) | collective-permute-done | bytes 2080 | tf_op jit(solution)/shard_map/ppermute | solution.py:199
  35.8 2.1 %collective-permute-start.13 = (f32[2,256]{1,0:T(2,128)S(1)}, f32[2,256]{1,0:T(2,128)S(1)}, u32[]{:S(2)}, u32[]{:S(2)}) collective-permute-start(f32[2,256]{1,0:T(2,128)S(1)} %add.9), channel_id=1, source_target_pairs={{0,4},{2,6},{4,0},{6,2},{8,12},{10,14},{12,8},{14,10},{1,5},{3,7},... | collective-permute-start | bytes 6152 | tf_op jit(solution)/shard_map/ppermute | solution.py:199
  37.8 1.6 %collective-permute-done.13 = f32[2,256]{1,0:T(2,128)S(1)} collective-permute-done((f32[2,256]{1,0:T(2,128)S(1)}, f32[2,256]{1,0:T(2,128)S(1)}, u32[]{:S(2)}, u32[]{:S(2)}) %collective-permute-start.13) | collective-permute-done | bytes 2080 | tf_op jit(solution)/shard_map/ppermute | solution.py:199
  39.4 3.0 %collective-permute-start.14 = (f32[2,256]{1,0:T(2,128)S(1)}, f32[2,256]{1,0:T(2,128)S(1)}, u32[]{:S(2)}, u32[]{:S(2)}) collective-permute-start(f32[2,256]{1,0:T(2,128)S(1)} %add.10), channel_id=1, source_target_pairs={{0,8},{2,10},{4,12},{6,14},{8,0},{10,2},{12,4},{14,6},{1,9},{3,11}... | collective-permute-start | bytes 6152 | tf_op jit(solution)/shard_map/ppermute | solution.py:199
  42.4 1.6 %collective-permute-done.14 = f32[2,256]{1,0:T(2,128)S(1)} collective-permute-done((f32[2,256]{1,0:T(2,128)S(1)}, f32[2,256]{1,0:T(2,128)S(1)}, u32[]{:S(2)}, u32[]{:S(2)}) %collective-permute-start.14) | collective-permute-done | bytes 2080 | tf_op jit(solution)/shard_map/ppermute | solution.py:199
  44.0 0.6 %add.11 = f32[2,256]{1,0:T(2,128)} add(f32[2,256]{1,0:T(2,128)S(1)} %add.10, f32[2,256]{1,0:T(2,128)S(1)} %collective-permute-done.14) | non-fusion elementwise | flops 512 | bytes 6144 | tf_op jit(solution)/shard_map/add | solution.py:199
  (2 shorter events, 0.0 us)
Async XLA Ops:
  0.6 26.7 %collective-permute-start = (bf16[2,8,256,256]{3,2,1,0:T(8,128)(2,1)}, bf16[2,8,256,256]{3,2,1,0:T(8,128)(2,1)S(1)}, u32[]{:S(2)}, u32[]{:S(2)}) collective-permute-start(bf16[2,8,256,256]{3,2,1,0:T(8,128)(2,1)} %source.1), channel_id=1, source_target_pairs={{0,1},{1,0},{2,3},{3,2},{4,5},{5,4},{6,7},{7,6},{8,9},{9,8},{10,11... | collective-permute-start | bytes 6291464 | tf_op jit(solution)/shard_map/ppermute | solution.py:125
  1.2 4.4 %collective-permute-start.2 = (bf16[2,1,256,256]{3,2,1,0:T(8,128)(2,1)}, bf16[2,1,256,256]{3,2,1,0:T(8,128)(2,1)S(1)}, u32[]{:S(2)}, u32[]{:S(2)}) collective-permute-start(bf16[2,1,256,256]{3,2,1,0:T(8,128)(2,1)} %refs_0_.1), channel_id=1, source_target_pairs={{0,1},{1,0},{2,3},{3,2},{4,5},{5,4},{6,7},{7,6},{8,9},{9,8},{10,11... | collective-permute-start | bytes 786440 | tf_op jit(solution)/shard_map/ppermute | solution.py:125
  1.3 7.5 %collective-permute-start.1 = (bf16[2,1,256,256]{3,2,1,0:T(8,128)(2,1)}, bf16[2,1,256,256]{3,2,1,0:T(8,128)(2,1)S(1)}, u32[]{:S(2)}, u32[]{:S(2)}) collective-permute-start(bf16[2,1,256,256]{3,2,1,0:T(8,128)(2,1)} %refs_0_.1), channel_id=1, source_target_pairs={{0,4},{1,3},{4,8},{5,1},{8,12},{9,5},{12,14},{13,9},{14,10},{15,13... | collective-permute-start | bytes 786440 | tf_op jit(solution)/shard_map/ppermute | solution.py:122
  5.6 7.2 %collective-permute-start.3 = (bf16[2,1,256,256]{3,2,1,0:T(8,128)(2,1)S(1)}, bf16[2,1,256,256]{3,2,1,0:T(8,128)(2,1)S(1)}, u32[]{:S(2)}, u32[]{:S(2)}) collective-permute-start(bf16[2,1,256,256]{3,2,1,0:T(8,128)(2,1)S(1)} %collective-permute-done.2), channel_id=1, source_target_pairs={{0,4},{1,3},{4,8},{5,1},{8,12},{9,5},{12,14},{13,9},{14,10},{15,13... | collective-permute-start | bytes 786440 | tf_op jit(solution)/shard_map/ppermute | solution.py:122
  8.8 6.8 %collective-permute-start.5 = (bf16[2,1,256,256]{3,2,1,0:T(8,128)(2,1)S(1)}, bf16[2,1,256,256]{3,2,1,0:T(8,128)(2,1)S(1)}, u32[]{:S(2)}, u32[]{:S(2)}) collective-permute-start(bf16[2,1,256,256]{3,2,1,0:T(8,128)(2,1)S(1)} %collective-permute-done.1.refs_1_), channel_id=1, source_target_pairs={{0,4},{1,3},{4,8},{5,1},{8,12},{9,5},{12,14},{13,9},{14,10},{15,13... | collective-permute-start | bytes 786440 | tf_op jit(solution)/shard_map/ppermute | solution.py:122
  12.8 6.4 %collective-permute-start.6 = (bf16[2,1,256,256]{3,2,1,0:T(8,128)(2,1)S(1)}, bf16[2,1,256,256]{3,2,1,0:T(8,128)(2,1)S(1)}, u32[]{:S(2)}, u32[]{:S(2)}) collective-permute-start(bf16[2,1,256,256]{3,2,1,0:T(8,128)(2,1)S(1)} %collective-permute-done.3), channel_id=1, source_target_pairs={{0,4},{1,3},{4,8},{5,1},{8,12},{9,5},{12,14},{13,9},{14,10},{15,13... | collective-permute-start | bytes 786440 | tf_op jit(solution)/shard_map/ppermute | solution.py:122
  15.6 6.4 %collective-permute-start.8 = (bf16[2,1,256,256]{3,2,1,0:T(8,128)(2,1)S(1)}, bf16[2,1,256,256]{3,2,1,0:T(8,128)(2,1)S(1)}, u32[]{:S(2)}, u32[]{:S(2)}) collective-permute-start(bf16[2,1,256,256]{3,2,1,0:T(8,128)(2,1)S(1)} %collective-permute-done.5.refs_3_), channel_id=1, source_target_pairs={{0,4},{1,3},{4,8},{5,1},{8,12},{9,5},{12,14},{13,9},{14,10},{15,13... | collective-permute-start | bytes 786440 | tf_op jit(solution)/shard_map/ppermute | solution.py:122
  19.2 6.4 %collective-permute-start.9 = (bf16[2,1,256,256]{3,2,1,0:T(8,128)(2,1)S(1)}, bf16[2,1,256,256]{3,2,1,0:T(8,128)(2,1)S(1)}, u32[]{:S(2)}, u32[]{:S(2)}) collective-permute-start(bf16[2,1,256,256]{3,2,1,0:T(8,128)(2,1)S(1)} %collective-permute-done.6), channel_id=1, source_target_pairs={{0,4},{1,3},{4,8},{5,1},{8,12},{9,5},{12,14},{13,9},{14,10},{15,13... | collective-permute-start | bytes 786440 | tf_op jit(solution)/shard_map/ppermute | solution.py:122
  21.2 6.1 %collective-permute-start.4 = (bf16[2,1,256,256]{3,2,1,0:T(8,128)(2,1)S(1)}, bf16[2,1,256,256]{3,2,1,0:T(8,128)(2,1)S(1)}, u32[]{:S(2)}, u32[]{:S(2)}) collective-permute-start(bf16[2,1,256,256]{3,2,1,0:T(8,128)(2,1)S(1)} %collective-permute-done.3), channel_id=1, source_target_pairs={{0,1},{1,0},{2,3},{3,2},{4,5},{5,4},{6,7},{7,6},{8,9},{9,8},{10,11... | collective-permute-start | bytes 786440 | tf_op jit(solution)/shard_map/ppermute | solution.py:125
  21.2 6.1 %collective-permute-start.7 = (bf16[2,1,256,256]{3,2,1,0:T(8,128)(2,1)S(1)}, bf16[2,1,256,256]{3,2,1,0:T(8,128)(2,1)S(1)}, u32[]{:S(2)}, u32[]{:S(2)}) collective-permute-start(bf16[2,1,256,256]{3,2,1,0:T(8,128)(2,1)S(1)} %collective-permute-done.6), channel_id=1, source_target_pairs={{0,1},{1,0},{2,3},{3,2},{4,5},{5,4},{6,7},{7,6},{8,9},{9,8},{10,11... | collective-permute-start | bytes 786440 | tf_op jit(solution)/shard_map/ppermute | solution.py:125
  22.0 8.0 %collective-permute-start.11 = (bf16[2,1,256,256]{3,2,1,0:T(8,128)(2,1)S(1)}, bf16[2,1,256,256]{3,2,1,0:T(8,128)(2,1)S(1)}, u32[]{:S(2)}, u32[]{:S(2)}) collective-permute-start(bf16[2,1,256,256]{3,2,1,0:T(8,128)(2,1)S(1)} %collective-permute-done.8.refs_5_), channel_id=1, source_target_pairs={{0,4},{1,3},{4,8},{5,1},{8,12},{9,5},{12,14},{13,9},{14,10},{15,13... | collective-permute-start | bytes 786440 | tf_op jit(solution)/shard_map/ppermute | solution.py:122
  25.5 4.5 %collective-permute-start.10 = (bf16[2,1,256,256]{3,2,1,0:T(8,128)(2,1)S(1)}, bf16[2,1,256,256]{3,2,1,0:T(8,128)(2,1)S(1)}, u32[]{:S(2)}, u32[]{:S(2)}) collective-permute-start(bf16[2,1,256,256]{3,2,1,0:T(8,128)(2,1)S(1)} %collective-permute-done.9), channel_id=1, source_target_pairs={{0,1},{1,0},{2,3},{3,2},{4,5},{5,4},{6,7},{7,6},{8,9},{9,8},{10,11... | collective-permute-start | bytes 786440 | tf_op jit(solution)/shard_map/ppermute | solution.py:125
  25.5 1.6 %copy-start = (bf16[2,8,256,256]{3,2,1,0:T(8,128)(2,1)S(1)}, bf16[2,8,256,256]{3,2,1,0:T(8,128)(2,1)}, u32[]{:S(2)}) copy-start(bf16[2,8,256,256]{3,2,1,0:T(8,128)(2,1)} %source.1) | copy-start | bytes 6291460
  27.1 0.9 %copy-start.1 = (bf16[2,1,256,256]{3,2,1,0:T(8,128)(2,1)S(1)}, bf16[2,1,256,256]{3,2,1,0:T(8,128)(2,1)}, u32[]{:S(2)}) copy-start(bf16[2,1,256,256]{3,2,1,0:T(8,128)(2,1)} %refs_0_.1) | copy-start | bytes 786436
  27.1 1.0 %copy-start.2 = (s32[2,8]{1,0:T(2,128)S(1)}, s32[2,8]{1,0:T(2,128)}, u32[]{:S(2)}) copy-start(s32[2,8]{1,0:T(2,128)} %structure.3) | copy-start | bytes 196
  27.1 1.0 %copy-start.4 = (s32[16]{0:T(128)S(1)}, s32[16]{0:T(128)}, u32[]{:S(2)}) copy-start(s32[16]{0:T(128)} %block_slot.3) | copy-start | bytes 196
  27.3 2.7 %copy-start.3 = (f32[2,256]{1,0:T(2,128)S(1)}, f32[2,256]{1,0:T(2,128)}, u32[]{:S(2)}) copy-start(f32[2,256]{1,0:T(2,128)} %diag.1) | copy-start | bytes 6148
  32.2 3.6 %collective-permute-start.12 = (f32[2,256]{1,0:T(2,128)S(1)}, f32[2,256]{1,0:T(2,128)S(1)}, u32[]{:S(2)}, u32[]{:S(2)}) collective-permute-start(f32[2,256]{1,0:T(2,128)S(1)} %get-tuple-element.9), channel_id=1, source_target_pairs={{0,2},{2,0},{4,6},{6,4},{8,10},{10,8},{12,14},{14,12},{1,3},{3,1},... | collective-permute-start | bytes 6152 | tf_op jit(solution)/shard_map/ppermute | solution.py:199
  35.8 3.6 %collective-permute-start.13 = (f32[2,256]{1,0:T(2,128)S(1)}, f32[2,256]{1,0:T(2,128)S(1)}, u32[]{:S(2)}, u32[]{:S(2)}) collective-permute-start(f32[2,256]{1,0:T(2,128)S(1)} %add.9), channel_id=1, source_target_pairs={{0,4},{2,6},{4,0},{6,2},{8,12},{10,14},{12,8},{14,10},{1,5},{3,7},... | collective-permute-start | bytes 6152 | tf_op jit(solution)/shard_map/ppermute | solution.py:199
  39.4 4.6 %collective-permute-start.14 = (f32[2,256]{1,0:T(2,128)S(1)}, f32[2,256]{1,0:T(2,128)S(1)}, u32[]{:S(2)}, u32[]{:S(2)}) collective-permute-start(f32[2,256]{1,0:T(2,128)S(1)} %add.10), channel_id=1, source_target_pairs={{0,8},{2,10},{4,12},{6,14},{8,0},{10,2},{12,4},{14,6},{1,9},{3,11}... | collective-permute-start | bytes 6152 | tf_op jit(solution)/shard_map/ppermute | solution.py:199

commit v3 on v2

v3 whole, which is shorter than its diff:
```python
import functools
import jax
import jax.numpy as jnp
from jax import lax
from jax.experimental import pallas as pl
from jax.experimental.pallas import tpu as pltpu
from jax.sharding import PartitionSpec as P

AXES = ("prow", "pcol")


def ring_order(size):
    return list(range(0, size, 2)) + [i for i in range(size - 1, 0, -1) if i % 2]


def ring_pairs(size):
    order = ring_order(size)
    pairs = []
    for place, row in enumerate(order):
        pairs.append((row * 2, order[(place + 1) % size] * 2))
        pairs.append((row * 2 + 1, order[(place - 1) % size] * 2 + 1))
    return pairs


class Place:
    def __init__(self, size):
        self.size = size
        self.prow = lax.axis_index("prow")
        self.pcol = lax.axis_index("pcol")
        odd = self.prow & 1
        half = self.prow >> 1
        self.at = half + odd * (size - 1 - 2 * half)

    def row(self, steps):
        if steps == 0:
            return self.prow
        at = lax.rem(self.at + self.size - steps * (1 - 2 * self.pcol), self.size)
        return jnp.where(2 * at < self.size, 2 * at, 2 * (self.size - 1 - at) + 1)


def load_kernel(source, target, sem):
    copy = pltpu.make_async_copy(source, target, sem)
    copy.start()
    copy.wait()


def prepare_kernel(grid_rows, s, late, structure, block_slot, own, other, late_tiles, marks):
    place = Place(grid_rows)
    rows, cols, size = own.shape[0], own.shape[1], own.shape[2]
    count = late_tiles.shape[0]
    per = count // len(late)
    slots = [block_slot[structure[s, place.row(k) * per + i]] for k in late for i in range(per)]
    every = [block_slot[structure[s, b]] for b in range(structure.shape[1])]
    for r in range(rows):
        row = place.prow * rows + r
        used = functools.reduce(jnp.logical_or, [slot == row for slot in every])
        marks[pl.ds(r, 1)] = jnp.full((1, size), -used.astype(jnp.float32))
        for i, slot in enumerate(slots):
            hit = (slot == row).astype(jnp.float32)
            marks[pl.ds(rows + i * rows + r, 1)] = jnp.full((1, size), hit)
    for i, slot in enumerate(slots):
        at = lax.rem(slot, cols)
        for r in range(rows):
            late_tiles[i, pl.ds(r * size, size)] = jnp.where(slot // cols == place.pcol, own[r, at], other[r, at])


def add_kernel(grid_rows, steps, fresh, structure, block_slot, own, other, *refs):
    panels, (acc, own_panel) = refs[:len(steps)], refs[-2:]
    place = Place(grid_rows)
    rows, cols, size = own.shape[0], own.shape[1], own.shape[2]
    supers, per = panels[0].shape[0], panels[0].shape[1]
    if fresh:
        own_panel[...] = jnp.zeros_like(own_panel)
    shard_rows = [place.row(k) * per for k in steps]
    blocks = [(panel, k) for panel in panels for k in range(per)]
    slots = [[block_slot[structure[s, at + k]] for at in shard_rows for k in range(per)] for s in range(supers)]
    for s in range(supers):
        for r in range(rows):
            for slot, (panel, k) in zip(slots[s], blocks):

                @pl.when(slot == place.prow * rows + r)
                def _():
                    own_panel[s, pl.ds(r * size, size)] = panel[s, k]

    for s in range(supers):
        for r in range(rows):
            here = pl.ds(r * size, size)
            total = None if fresh else acc[s, here]
            for slot, (panel, k) in zip(slots[s], blocks):
                at = lax.rem(slot, cols)
                tile = jnp.where(slot // cols == place.pcol, own[r, at], other[r, at])
                part = jnp.dot(tile, panel[s, k], preferred_element_type=jnp.float32)
                total = part if total is None else total + part
            acc[s, here] = total


def finish_kernel(supers, count, diag, first, acc, own_panel, *refs):
    tiles, marks, refs = refs[:supers], refs[supers:2 * supers], refs[2 * supers:]
    panels, (sigma, value) = refs[:-2], refs[-2:]
    rows, size = sigma.shape[1], sigma.shape[2]
    blocks = [(panel, k) for panel in panels for k in range(count // len(panels))]
    for s in range(supers):
        result = diag[pl.ds(s, 1)] * first[...]
        for r in range(rows):
            here = pl.ds(r * size, size)
            total = acc[s, here]
            for i, (panel, k) in enumerate(blocks):
                total = total + jnp.dot(tiles[s][i, here], panel[s, k], preferred_element_type=jnp.float32)
            total = total * marks[s][pl.ds(r, 1)]
            sigma[s, r] = total.astype(sigma.dtype)
            weight = own_panel[s, here].astype(jnp.float32)
            for i, (panel, k) in enumerate(blocks):
                weight = weight + marks[s][pl.ds(rows + i * rows + r, 1)] * panel[s, k].astype(jnp.float32)
            result = result - jnp.sum(weight * total, axis=0, keepdims=True)
        value[pl.ds(s, 1)] = result


def per_device(grid_rows, inverse_tiles, panel_blocks, diag_inverse, structure, block_slot):
    rows, size = inverse_tiles.shape[0], inverse_tiles.shape[2]
    supers, per = panel_blocks.shape[0], panel_blocks.shape[1]
    pairs = ring_pairs(grid_rows)
    swap = [(i, i ^ 1) for i in range(2 * grid_rows)]
    ways, backs = grid_rows // 2, (grid_rows - 1) // 2

    def hop(x):
        return lax.ppermute(x, AXES, pairs)

    def cross(x):
        return lax.ppermute(x, AXES, swap)

    smem = pl.BlockSpec(memory_space=pltpu.SMEM)
    vmem = pl.BlockSpec(memory_space=pltpu.VMEM)
    hbm = pl.BlockSpec(memory_space=pltpu.HBM)

    mine = hop(panel_blocks)
    theirs = cross(panel_blocks)
    own = pl.pallas_call(
        load_kernel,
        out_shape=jax.ShapeDtypeStruct(inverse_tiles.shape, inverse_tiles.dtype),
        in_specs=[hbm],
        out_specs=vmem,
        scratch_shapes=[pltpu.SemaphoreType.DMA],
        compiler_params=pltpu.CompilerParams(vmem_limit_bytes=4 << 20),
        name="load",
    )(inverse_tiles)
    other = cross(inverse_tiles)
    shards = [(0, panel_blocks), (1, mine)]
    for step in range(1, ways + 1):
        if step <= backs:
            theirs = hop(theirs)
        if step < ways:
            mine = hop(mine)
        if step <= backs:
            shards.append((-step, cross(theirs)))
        if step < ways:
            shards.append((step + 1, mine))
    late = [shard for shard in shards if shard[0] in (ways, -backs)]
    tail = len(late)

    tile = size * size
    small = pltpu.CompilerParams(vmem_limit_bytes=8 << 20)
    shape = jax.ShapeDtypeStruct
    sums = ()
    for step in range(2, ways + 1):
        batch = [x for x in shards if x[0] in ((0, 1) if step == 2 else (step - 1, 2 - step))]
        sums = pl.pallas_call(
            functools.partial(add_kernel, grid_rows, [k for k, _ in batch], not sums),
            out_shape=(
                shape((supers, rows * size, size), jnp.float32),
                shape((supers, rows * size, size), jnp.bfloat16),
            ),
            in_specs=[smem] * 2 + [vmem] * (2 + len(batch) + len(sums)),
            out_specs=(vmem, vmem),
            input_output_aliases={4 + len(batch) + i: i for i in range(len(sums))},
            compiler_params=small,
            cost_estimate=pl.CostEstimate(
                flops=2 * supers * len(batch) * per * rows * tile * size,
                bytes_accessed=2 * supers * len(batch) * per * (rows + 1) * tile,
                transcendentals=0,
            ),
            name="add",
        )(structure, block_slot, own, other, *[x for _, x in batch], *sums)
    tiles, marks = [], []
    for sup in range(supers):
        made = pl.pallas_call(
            functools.partial(prepare_kernel, grid_rows, sup, [k for k, _ in late]),
            out_shape=(
                shape((tail * per, rows * size, size), jnp.bfloat16),
                shape((rows + tail * per * rows, size), jnp.float32),
            ),
            in_specs=[smem] * 2 + [vmem] * 2,
            out_specs=(vmem,) * 2,
            compiler_params=small,
            cost_estimate=pl.CostEstimate(
                flops=0, bytes_accessed=4 * tail * per * rows * tile, transcendentals=0
            ),
            name="prepare",
        )(structure, block_slot, own, other)
        tiles.append(made[0])
        marks.append(made[1])
    first = jnp.full((1, size), lax.axis_index("prow") == 0, jnp.float32)

    sigma, value = pl.pallas_call(
        functools.partial(finish_kernel, supers, tail * per),
        out_shape=(
            shape((supers, rows, size, size), jnp.bfloat16),
            shape(diag_inverse.shape, jnp.float32),
        ),
        in_specs=[vmem] * (4 + 2 * supers + tail),
        out_specs=(vmem, vmem),
        compiler_params=small,
        cost_estimate=pl.CostEstimate(
            flops=2 * supers * tail * per * rows * tile * size,
            bytes_accessed=supers * rows * tile * 8,
            transcendentals=0,
        ),
        name="finish",
    )(diag_inverse, first, *sums, *tiles, *marks, *[x for _, x in late])

    sigma = pl.pallas_call(
        load_kernel,
        out_shape=shape(sigma.shape, sigma.dtype),
        in_specs=[vmem],
        out_specs=hbm,
        scratch_shapes=[pltpu.SemaphoreType.DMA],
        compiler_params=pltpu.CompilerParams(vmem_limit_bytes=4 << 20),
        name="store",
    )(sigma)

    stride = 1
    while stride < grid_rows:
        value = value + lax.ppermute(value, "prow", [(i, i ^ stride) for i in range(grid_rows)])
        stride *= 2
    return sigma, value


def solution(mesh):
    in_specs = (
        P(("fields", "prow"), "pcol", None, None),
        P("fields", "prow", None, "pcol"),
        P("fields", "pcol"),
        P("fields", None),
        P("fields"),
    )
    out_specs = (P("fields", "prow", None, "pcol"), P("fields", "pcol"))
    grid_rows = mesh.shape["prow"]

    def body(*args):
        return per_device(grid_rows, *args)

    return jax.shard_map(body, mesh=mesh, in_specs=in_specs, out_specs=out_specs, check_vma=False)
```

time: 44.7 us -> 51.9 us (1.16)
  Pallas kernels: 4.19 us -> 11.3 us
    pallas_call x2 -> x7, Pallas kernels: 4.04 us -> 11.2 us  [the longest x3 6.34 us: per_device(): pl.pallas_call(functools.partial(add_kernel, grid_rows, [k for k, _ in ba...]
    ppermute x3, waiting for transfers between devices: 4.69 us -> 3.88 us  [per_device(): lax.ppermute(value, 'prow', [(i, i ^ stride) for i in range(grid_rows)])]
    ppermute x7, waiting for transfers between devices: 6.13 us -> 6.86 us  [hop(): return lax.ppermute(x, AXES, pairs)]
  transfers between devices with their start and end apart: 15 -> 15, of which waited for: 10 -> 10; matrix products, arithmetic and copies ran while one was open for 0% -> 0% of each run, Pallas kernels for 5% -> 21%
where the time goes in v3:
time: 51.9 us; the launch traced here: 51.6 us
  starting transfers between devices  24.7 us (48%)
  waiting for transfers between devices  12.1 us (23%)
  Pallas kernels  11.3 us (22%)
  local copies, waits for them, and re-layouts  2.11 us (4%)
  between operations  0.79 us (2%)
  other arithmetic  0.59 us (1%)
    ppermute x7, starting transfers between devices, hop(): return lax.ppermute(x, AXES, pairs)  16.3 us
    ppermute x3, starting transfers between devices, per_device(): lax.ppermute(value, 'prow', [(i, i ^ stride) for i in range(grid_rows)])  7.19 us
    ppermute x7, waiting for transfers between devices, hop(): return lax.ppermute(x, AXES, pairs)  6.86 us
    pallas_call x3, Pallas kernels, per_device(): pl.pallas_call(functools.partial(add_kernel, grid_rows, [k for k, _ in ba...  6.34 us
    ppermute x3, waiting for transfers between devices, per_device(): lax.ppermute(value, 'prow', [(i, i ^ stride) for i in range(grid_rows)])  3.88 us
    pallas_call x2, Pallas kernels, per_device(): pl.pallas_call(functools.partial(prepare_kernel, grid_rows, sup, [k for k...  3.42 us
    unnamed x10, local copies, waits for them, and re-layouts  2.11 us
    ppermute x5, waiting for transfers between devices, cross(): return lax.ppermute(x, AXES, swap)  1.31 us
  transfers between devices with their start and end apart: 15, of which 10 were waited for; matrix products, arithmetic and copies ran while one was open for 0% of the time, Pallas kernels for 21%

profile of v3, /device:TPU:0, one launch (start us, length us, event | category | flops | bytes accessed | tf_op | source)
XLA Modules:
  0.0 51.6 jit_solution(325753764502989123)
XLA Ops:
  0.6 0.6 %collective-permute-start = (bf16[2,8,256,256]{3,2,1,0:T(8,128)(2,1)}, bf16[2,8,256,256]{3,2,1,0:T(8,128)(2,1)}, u32[]{:S(2)}, u32[]{:S(2)}) collective-permute-start(bf16[2,8,256,256]{3,2,1,0:T(8,128)(2,1)} %source.1), channel_id=1, source_target_pairs={{0,1},{1,0},{2,3},{3,2},{4,5},{5,4},{6,7},{7,6},{8,9},{9,8},{10,11... | collective-permute-start | bytes 6291464 | tf_op jit(solution)/shard_map/ppermute | solution.py:129
  1.2 0.1 collective-permute-start.1
  1.3 3.0 %collective-permute-start.5 = (bf16[2,1,256,256]{3,2,1,0:T(8,128)(2,1)}, bf16[2,1,256,256]{3,2,1,0:T(8,128)(2,1)S(1)}, u32[]{:S(2)}, u32[]{:S(2)}) collective-permute-start(bf16[2,1,256,256]{3,2,1,0:T(8,128)(2,1)} %refs_0_.1), channel_id=1, source_target_pairs={{0,4},{1,3},{4,8},{5,1},{8,12},{9,5},{12,14},{13,9},{14,10},{15,13... | collective-permute-start | bytes 786440 | tf_op jit(solution)/shard_map/ppermute | solution.py:126
  4.3 1.3 %collective-permute-done.1 = bf16[2,1,256,256]{3,2,1,0:T(8,128)(2,1)S(1)} collective-permute-done((bf16[2,1,256,256]{3,2,1,0:T(8,128)(2,1)}, bf16[2,1,256,256]{3,2,1,0:T(8,128)(2,1)S(1)}, u32[]{:S(2)}, u32[]{:S(2)}) %collective-permute-start.1) | collective-permute-done | bytes 262176 | tf_op jit(solution)/shard_map/ppermute | solution.py:129
  5.6 2.9 %collective-permute-start.2 = (bf16[2,1,256,256]{3,2,1,0:T(8,128)(2,1)S(1)}, bf16[2,1,256,256]{3,2,1,0:T(8,128)(2,1)}, u32[]{:S(2)}, u32[]{:S(2)}) collective-permute-start(bf16[2,1,256,256]{3,2,1,0:T(8,128)(2,1)S(1)} %collective-permute-done.1), channel_id=1, source_target_pairs={{0,4},{1,3},{4,8},{5,1},{8,12},{9,5},{12,14},{13,9},{14,10},{15,13... | collective-permute-start | bytes 786440 | tf_op jit(solution)/shard_map/ppermute | solution.py:126
  8.5 0.3 collective-permute-done.5.refs_1_
  8.8 2.1 %collective-permute-start.6 = (bf16[2,1,256,256]{3,2,1,0:T(8,128)(2,1)S(1)}, bf16[2,1,256,256]{3,2,1,0:T(8,128)(2,1)S(1)}, u32[]{:S(2)}, u32[]{:S(2)}) collective-permute-start(bf16[2,1,256,256]{3,2,1,0:T(8,128)(2,1)S(1)} %collective-permute-done.5.refs_1_), channel_id=1, source_target_pairs={{0,4},{1,3},{4,8},{5,1},{8,12},{9,5},{12,14},{13,9},{14,10},{15,13... | collective-permute-start | bytes 786440 | tf_op jit(solution)/shard_map/ppermute | solution.py:126
  10.8 2.0 %collective-permute-done.2 = bf16[2,1,256,256]{3,2,1,0:T(8,128)(2,1)} collective-permute-done((bf16[2,1,256,256]{3,2,1,0:T(8,128)(2,1)S(1)}, bf16[2,1,256,256]{3,2,1,0:T(8,128)(2,1)}, u32[]{:S(2)}, u32[]{:S(2)}) %collective-permute-start.2) | collective-permute-done | bytes 262176 | tf_op jit(solution)/shard_map/ppermute | solution.py:126
  12.9 2.1 %collective-permute-start.3 = (bf16[2,1,256,256]{3,2,1,0:T(8,128)(2,1)}, bf16[2,1,256,256]{3,2,1,0:T(8,128)(2,1)}, u32[]{:S(2)}, u32[]{:S(2)}) collective-permute-start(bf16[2,1,256,256]{3,2,1,0:T(8,128)(2,1)} %collective-permute-done.2), channel_id=1, source_target_pairs={{0,4},{1,3},{4,8},{5,1},{8,12},{9,5},{12,14},{13,9},{14,10},{15,13... | collective-permute-start | bytes 786440 | tf_op jit(solution)/shard_map/ppermute | solution.py:126
  15.0 0.6 %collective-permute-done.6.refs_1_ = bf16[2,1,256,256]{3,2,1,0:T(8,128)(2,1)S(1)} collective-permute-done((bf16[2,1,256,256]{3,2,1,0:T(8,128)(2,1)S(1)}, bf16[2,1,256,256]{3,2,1,0:T(8,128)(2,1)S(1)}, u32[]{:S(2)}, u32[]{:S(2)}) %collective-permute-start.6) | collective-permute-done | bytes 262176 | tf_op jit(solution)/shard_map/ppermute | solution.py:126
  15.6 2.1 %collective-permute-start.7 = (bf16[2,1,256,256]{3,2,1,0:T(8,128)(2,1)S(1)}, bf16[2,1,256,256]{3,2,1,0:T(8,128)(2,1)S(1)}, u32[]{:S(2)}, u32[]{:S(2)}) collective-permute-start(bf16[2,1,256,256]{3,2,1,0:T(8,128)(2,1)S(1)} %collective-permute-done.6.refs_1_), channel_id=1, source_target_pairs={{0,4},{1,3},{4,8},{5,1},{8,12},{9,5},{12,14},{13,9},{14,10},{15,13... | collective-permute-start | bytes 786440 | tf_op jit(solution)/shard_map/ppermute | solution.py:126
  17.7 1.9 %collective-permute-done.3 = bf16[2,1,256,256]{3,2,1,0:T(8,128)(2,1)} collective-permute-done((bf16[2,1,256,256]{3,2,1,0:T(8,128)(2,1)}, bf16[2,1,256,256]{3,2,1,0:T(8,128)(2,1)}, u32[]{:S(2)}, u32[]{:S(2)}) %collective-permute-start.3) | collective-permute-done | bytes 262176 | tf_op jit(solution)/shard_map/ppermute | solution.py:126
  19.6 2.1 %collective-permute-start.9 = (bf16[2,1,256,256]{3,2,1,0:T(8,128)(2,1)}, bf16[2,1,256,256]{3,2,1,0:T(8,128)(2,1)}, u32[]{:S(2)}, u32[]{:S(2)}) collective-permute-start(bf16[2,1,256,256]{3,2,1,0:T(8,128)(2,1)} %collective-permute-done.3), channel_id=1, source_target_pairs={{0,4},{1,3},{4,8},{5,1},{8,12},{9,5},{12,14},{13,9},{14,10},{15,13... | collective-permute-start | bytes 786440 | tf_op jit(solution)/shard_map/ppermute | solution.py:126
  21.7 0.0 collective-permute-start.8
  21.7 0.5 collective-permute-start.4
  22.2 0.1 collective-permute-done.7.refs_1_
  22.3 2.1 %collective-permute-start.11 = (bf16[2,1,256,256]{3,2,1,0:T(8,128)(2,1)S(1)}, bf16[2,1,256,256]{3,2,1,0:T(8,128)(2,1)S(1)}, u32[]{:S(2)}, u32[]{:S(2)}) collective-permute-start(bf16[2,1,256,256]{3,2,1,0:T(8,128)(2,1)S(1)} %collective-permute-done.7.refs_1_), channel_id=1, source_target_pairs={{0,4},{1,3},{4,8},{5,1},{8,12},{9,5},{12,14},{13,9},{14,10},{15,13... | collective-permute-start | bytes 786440 | tf_op jit(solution)/shard_map/ppermute | solution.py:126
  24.4 1.9 %collective-permute-done.9 = bf16[2,1,256,256]{3,2,1,0:T(8,128)(2,1)} collective-permute-done((bf16[2,1,256,256]{3,2,1,0:T(8,128)(2,1)}, bf16[2,1,256,256]{3,2,1,0:T(8,128)(2,1)}, u32[]{:S(2)}, u32[]{:S(2)}) %collective-permute-start.9) | collective-permute-done | bytes 262176 | tf_op jit(solution)/shard_map/ppermute | solution.py:126
  26.3 0.0 collective-permute-start.10
  26.3 0.0 copy-start
  26.3 1.6 %copy-done = bf16[2,8,256,256]{3,2,1,0:T(8,128)(2,1)S(1)} copy-done((bf16[2,8,256,256]{3,2,1,0:T(8,128)(2,1)S(1)}, bf16[2,8,256,256]{3,2,1,0:T(8,128)(2,1)}, u32[]{:S(2)}) %copy-start) | copy-done | bytes 2097176
  27.9 0.0 copy-start.2
  27.9 0.1 load.1.own
  28.0 0.0 collective-permute-done.other
  28.0 0.5 copy-done.2
  28.5 0.0 copy-done.3
  28.5 1.7 %prepare.2 = (bf16[2,512,256]{2,1,0:T(8,128)(2,1)S(1)}, f32[6,256]{1,0:T(8,128)S(1)}) custom-call(s32[2,8]{1,0:T(2,128)S(1)} %copy-done.2, s32[16]{0:T(128)S(1)} %copy-done.3, bf16[2,8,256,256]{3,2,1,0:T(8,128)(2,1)S(1)} %load.1.own, bf16[2,8,256,256]{3,2,1,0:T(8,128)(2,1)} %collective-permute-done.other), custom_call_target="tpu_custom_call" | custom-call | bytes 1048576 | tf_op jit(solution)/shard_map/prepare/pallas_call | solution.py:185
  30.2 0.0 copy-start.1
  30.3 1.7 %prepare.3 = (bf16[2,512,256]{2,1,0:T(8,128)(2,1)S(1)}, f32[6,256]{1,0:T(8,128)S(1)}) custom-call(s32[2,8]{1,0:T(2,128)S(1)} %copy-done.2, s32[16]{0:T(128)S(1)} %copy-done.3, bf16[2,8,256,256]{3,2,1,0:T(8,128)(2,1)S(1)} %load.1.own, bf16[2,8,256,256]{3,2,1,0:T(8,128)(2,1)} %collective-permute-done.other), custom_call_target="tpu_custom_call" | custom-call | bytes 1048576 | tf_op jit(solution)/shard_map/prepare/pallas_call | solution.py:185
  32.0 0.0 copy-done.1
  32.0 2.1 %add.15 = (f32[2,512,256]{2,1,0:T(8,128)S(1)}, bf16[2,512,256]{2,1,0:T(8,128)(2,1)S(1)}) custom-call(s32[2,8]{1,0:T(2,128)S(1)} %copy-done.2, s32[16]{0:T(128)S(1)} %copy-done.3, bf16[2,8,256,256]{3,2,1,0:T(8,128)(2,1)S(1)} %load.1.own, bf16[2,8,256,256]{3,2,1,0:T(8,128)(2,1)} %collective-permute-done.other, bf16[2,1,256,256]{3,2,1,0:T(8,128)(2,1)S(1)} %copy-done.1, ...), custom_call_target="tpu_custom_call" | custom-call | flops 268435456 | bytes 1572864 | tf_op jit(solution)/shard_map/add/pallas_call | solution.py:166
  34.1 0.0 collective-permute-done.8.refs_0_
  34.1 2.1 %add.16 = (f32[2,512,256]{2,1,0:T(8,128)S(1)}, bf16[2,512,256]{2,1,0:T(8,128)(2,1)S(1)}) custom-call(s32[2,8]{1,0:T(2,128)S(1)} %copy-done.2, s32[16]{0:T(128)S(1)} %copy-done.3, bf16[2,8,256,256]{3,2,1,0:T(8,128)(2,1)S(1)} %load.1.own, bf16[2,8,256,256]{3,2,1,0:T(8,128)(2,1)} %collective-permute-done.other, ...), custom_call_target="tpu_custom_call", output_to_operand_aliasing={{0}: (6, {}), {1}: (7, {})} | custom-call | flops 268435456 | bytes 1572864 | tf_op jit(solution)/shard_map/add/pallas_call | solution.py:166
  36.3 0.0 collective-permute-done.4.refs_0_
  36.3 0.0 copy-start.4
  36.3 2.1 %add.17 = (f32[2,512,256]{2,1,0:T(8,128)S(1)}, bf16[2,512,256]{2,1,0:T(8,128)(2,1)S(1)}) custom-call(s32[2,8]{1,0:T(2,128)S(1)} %copy-done.2, s32[16]{0:T(128)S(1)} %copy-done.3, bf16[2,8,256,256]{3,2,1,0:T(8,128)(2,1)S(1)} %load.1.own, bf16[2,8,256,256]{3,2,1,0:T(8,128)(2,1)} %collective-permute-done.other, ...), custom_call_target="tpu_custom_call", output_to_operand_aliasing={{0}: (6, {}), {1}: (7, {})} | custom-call | flops 268435456 | bytes 1572864 | tf_op jit(solution)/shard_map/add/pallas_call | solution.py:166
  38.4 0.0 collective-permute-done.11.refs_5_
  38.4 0.0 collective-permute-done.10.refs_4_
  38.4 0.0 copy-done.4
  38.5 0.6 %finish.1 = (bf16[2,2,256,256]{3,2,1,0:T(8,128)(2,1)S(1)}, f32[2,256]{1,0:T(2,128)S(1)}) custom-call(f32[2,256]{1,0:T(2,128)S(1)} %copy-done.4, f32[1,256]{1,0:T(1,128)S(1)} %broadcast_in_dim.3.first, f32[2,512,256]{2,1,0:T(8,128)S(1)} %get-tuple-element.18.acc, bf16[2,512,256]{2,1,0:T(8,128)(2,1)S(1)} %get-tuple-element.19.own_panel, ...), custom_call_target="tpu_custom_call" | custom-call | flops 268435456 | bytes 2097152 | tf_op jit(solution)/shard_map/finish/pallas_call | solution.py:203
  39.1 2.1 %collective-permute-start.12 = (f32[2,256]{1,0:T(2,128)S(1)}, f32[2,256]{1,0:T(2,128)S(1)}, u32[]{:S(2)}, u32[]{:S(2)}) collective-permute-start(f32[2,256]{1,0:T(2,128)S(1)} %get-tuple-element.25), channel_id=1, source_target_pairs={{0,2},{2,0},{4,6},{6,4},{8,10},{10,8},{12,14},{14,12},{1,3},{3,1},... | collective-permute-start | bytes 6152 | tf_op jit(solution)/shard_map/ppermute | solution.py:232
  41.2 1.6 %collective-permute-done.12 = f32[2,256]{1,0:T(2,128)S(1)} collective-permute-done((f32[2,256]{1,0:T(2,128)S(1)}, f32[2,256]{1,0:T(2,128)S(1)}, u32[]{:S(2)}, u32[]{:S(2)}) %collective-permute-start.12) | collective-permute-done | bytes 2080 | tf_op jit(solution)/shard_map/ppermute | solution.py:232
  42.7 2.1 %collective-permute-start.13 = (f32[2,256]{1,0:T(2,128)S(1)}, f32[2,256]{1,0:T(2,128)S(1)}, u32[]{:S(2)}, u32[]{:S(2)}) collective-permute-start(f32[2,256]{1,0:T(2,128)S(1)} %add.12), channel_id=1, source_target_pairs={{0,4},{2,6},{4,0},{6,2},{8,12},{10,14},{12,8},{14,10},{1,5},{3,7},... | collective-permute-start | bytes 6152 | tf_op jit(solution)/shard_map/ppermute | solution.py:232
  44.8 1.6 %collective-permute-done.13 = f32[2,256]{1,0:T(2,128)S(1)} collective-permute-done((f32[2,256]{1,0:T(2,128)S(1)}, f32[2,256]{1,0:T(2,128)S(1)}, u32[]{:S(2)}, u32[]{:S(2)}) %collective-permute-start.13) | collective-permute-done | bytes 2080 | tf_op jit(solution)/shard_map/ppermute | solution.py:232
  46.4 3.0 %collective-permute-start.14 = (f32[2,256]{1,0:T(2,128)S(1)}, f32[2,256]{1,0:T(2,128)S(1)}, u32[]{:S(2)}, u32[]{:S(2)}) collective-permute-start(f32[2,256]{1,0:T(2,128)S(1)} %add.13), channel_id=1, source_target_pairs={{0,8},{2,10},{4,12},{6,14},{8,0},{10,2},{12,4},{14,6},{1,9},{3,11}... | collective-permute-start | bytes 6152 | tf_op jit(solution)/shard_map/ppermute | solution.py:232
  49.4 0.8 %store.1 = bf16[2,2,256,256]{3,2,1,0:T(8,128)(2,1)} custom-call(bf16[2,2,256,256]{3,2,1,0:T(8,128)(2,1)S(1)} %get-tuple-element.24.source), custom_call_target="tpu_custom_call" | custom-call | tf_op jit(solution)/shard_map/store/pallas_call | solution.py:220
  50.2 0.8 %collective-permute-done.14 = f32[2,256]{1,0:T(2,128)S(1)} collective-permute-done((f32[2,256]{1,0:T(2,128)S(1)}, f32[2,256]{1,0:T(2,128)S(1)}, u32[]{:S(2)}, u32[]{:S(2)}) %collective-permute-start.14) | collective-permute-done | bytes 2080 | tf_op jit(solution)/shard_map/ppermute | solution.py:232
  51.0 0.6 %add.14 = f32[2,256]{1,0:T(2,128)} add(f32[2,256]{1,0:T(2,128)S(1)} %add.13, f32[2,256]{1,0:T(2,128)S(1)} %collective-permute-done.14) | non-fusion elementwise | flops 512 | bytes 6144 | tf_op jit(solution)/shard_map/add | solution.py:232
  (4 shorter events, 0.0 us)
Async XLA Ops:
  0.6 27.4 %collective-permute-start = (bf16[2,8,256,256]{3,2,1,0:T(8,128)(2,1)}, bf16[2,8,256,256]{3,2,1,0:T(8,128)(2,1)}, u32[]{:S(2)}, u32[]{:S(2)}) collective-permute-start(bf16[2,8,256,256]{3,2,1,0:T(8,128)(2,1)} %source.1), channel_id=1, source_target_pairs={{0,1},{1,0},{2,3},{3,2},{4,5},{5,4},{6,7},{7,6},{8,9},{9,8},{10,11... | collective-permute-start | bytes 6291464 | tf_op jit(solution)/shard_map/ppermute | solution.py:129
  1.2 4.4 %collective-permute-start.1 = (bf16[2,1,256,256]{3,2,1,0:T(8,128)(2,1)}, bf16[2,1,256,256]{3,2,1,0:T(8,128)(2,1)S(1)}, u32[]{:S(2)}, u32[]{:S(2)}) collective-permute-start(bf16[2,1,256,256]{3,2,1,0:T(8,128)(2,1)} %refs_0_.1), channel_id=1, source_target_pairs={{0,1},{1,0},{2,3},{3,2},{4,5},{5,4},{6,7},{7,6},{8,9},{9,8},{10,11... | collective-permute-start | bytes 786440 | tf_op jit(solution)/shard_map/ppermute | solution.py:129
  1.3 7.5 %collective-permute-start.5 = (bf16[2,1,256,256]{3,2,1,0:T(8,128)(2,1)}, bf16[2,1,256,256]{3,2,1,0:T(8,128)(2,1)S(1)}, u32[]{:S(2)}, u32[]{:S(2)}) collective-permute-start(bf16[2,1,256,256]{3,2,1,0:T(8,128)(2,1)} %refs_0_.1), channel_id=1, source_target_pairs={{0,4},{1,3},{4,8},{5,1},{8,12},{9,5},{12,14},{13,9},{14,10},{15,13... | collective-permute-start | bytes 786440 | tf_op jit(solution)/shard_map/ppermute | solution.py:126
  5.6 7.3 %collective-permute-start.2 = (bf16[2,1,256,256]{3,2,1,0:T(8,128)(2,1)S(1)}, bf16[2,1,256,256]{3,2,1,0:T(8,128)(2,1)}, u32[]{:S(2)}, u32[]{:S(2)}) collective-permute-start(bf16[2,1,256,256]{3,2,1,0:T(8,128)(2,1)S(1)} %collective-permute-done.1), channel_id=1, source_target_pairs={{0,4},{1,3},{4,8},{5,1},{8,12},{9,5},{12,14},{13,9},{14,10},{15,13... | collective-permute-start | bytes 786440 | tf_op jit(solution)/shard_map/ppermute | solution.py:126
  8.8 6.8 %collective-permute-start.6 = (bf16[2,1,256,256]{3,2,1,0:T(8,128)(2,1)S(1)}, bf16[2,1,256,256]{3,2,1,0:T(8,128)(2,1)S(1)}, u32[]{:S(2)}, u32[]{:S(2)}) collective-permute-start(bf16[2,1,256,256]{3,2,1,0:T(8,128)(2,1)S(1)} %collective-permute-done.5.refs_1_), channel_id=1, source_target_pairs={{0,4},{1,3},{4,8},{5,1},{8,12},{9,5},{12,14},{13,9},{14,10},{15,13... | collective-permute-start | bytes 786440 | tf_op jit(solution)/shard_map/ppermute | solution.py:126
  12.9 6.7 %collective-permute-start.3 = (bf16[2,1,256,256]{3,2,1,0:T(8,128)(2,1)}, bf16[2,1,256,256]{3,2,1,0:T(8,128)(2,1)}, u32[]{:S(2)}, u32[]{:S(2)}) collective-permute-start(bf16[2,1,256,256]{3,2,1,0:T(8,128)(2,1)} %collective-permute-done.2), channel_id=1, source_target_pairs={{0,4},{1,3},{4,8},{5,1},{8,12},{9,5},{12,14},{13,9},{14,10},{15,13... | collective-permute-start | bytes 786440 | tf_op jit(solution)/shard_map/ppermute | solution.py:126
  15.6 6.7 %collective-permute-start.7 = (bf16[2,1,256,256]{3,2,1,0:T(8,128)(2,1)S(1)}, bf16[2,1,256,256]{3,2,1,0:T(8,128)(2,1)S(1)}, u32[]{:S(2)}, u32[]{:S(2)}) collective-permute-start(bf16[2,1,256,256]{3,2,1,0:T(8,128)(2,1)S(1)} %collective-permute-done.6.refs_1_), channel_id=1, source_target_pairs={{0,4},{1,3},{4,8},{5,1},{8,12},{9,5},{12,14},{13,9},{14,10},{15,13... | collective-permute-start | bytes 786440 | tf_op jit(solution)/shard_map/ppermute | solution.py:126
  19.6 6.7 %collective-permute-start.9 = (bf16[2,1,256,256]{3,2,1,0:T(8,128)(2,1)}, bf16[2,1,256,256]{3,2,1,0:T(8,128)(2,1)}, u32[]{:S(2)}, u32[]{:S(2)}) collective-permute-start(bf16[2,1,256,256]{3,2,1,0:T(8,128)(2,1)} %collective-permute-done.3), channel_id=1, source_target_pairs={{0,4},{1,3},{4,8},{5,1},{8,12},{9,5},{12,14},{13,9},{14,10},{15,13... | collective-permute-start | bytes 786440 | tf_op jit(solution)/shard_map/ppermute | solution.py:126
  21.7 12.5 %collective-permute-start.8 = (bf16[2,1,256,256]{3,2,1,0:T(8,128)(2,1)}, bf16[2,1,256,256]{3,2,1,0:T(8,128)(2,1)}, u32[]{:S(2)}, u32[]{:S(2)}) collective-permute-start(bf16[2,1,256,256]{3,2,1,0:T(8,128)(2,1)} %collective-permute-done.2), channel_id=1, source_target_pairs={{0,1},{1,0},{2,3},{3,2},{4,5},{5,4},{6,7},{7,6},{8,9},{9,8},{10,11... | collective-permute-start | bytes 786440 | tf_op jit(solution)/shard_map/ppermute | solution.py:129
  21.7 14.6 %collective-permute-start.4 = (bf16[2,1,256,256]{3,2,1,0:T(8,128)(2,1)}, bf16[2,1,256,256]{3,2,1,0:T(8,128)(2,1)}, u32[]{:S(2)}, u32[]{:S(2)}) collective-permute-start(bf16[2,1,256,256]{3,2,1,0:T(8,128)(2,1)} %collective-permute-done.3), channel_id=1, source_target_pairs={{0,1},{1,0},{2,3},{3,2},{4,5},{5,4},{6,7},{7,6},{8,9},{9,8},{10,11... | collective-permute-start | bytes 786440 | tf_op jit(solution)/shard_map/ppermute | solution.py:129
  22.3 16.1 %collective-permute-start.11 = (bf16[2,1,256,256]{3,2,1,0:T(8,128)(2,1)S(1)}, bf16[2,1,256,256]{3,2,1,0:T(8,128)(2,1)S(1)}, u32[]{:S(2)}, u32[]{:S(2)}) collective-permute-start(bf16[2,1,256,256]{3,2,1,0:T(8,128)(2,1)S(1)} %collective-permute-done.7.refs_1_), channel_id=1, source_target_pairs={{0,4},{1,3},{4,8},{5,1},{8,12},{9,5},{12,14},{13,9},{14,10},{15,13... | collective-permute-start | bytes 786440 | tf_op jit(solution)/shard_map/ppermute | solution.py:126
  26.3 12.2 %collective-permute-start.10 = (bf16[2,1,256,256]{3,2,1,0:T(8,128)(2,1)}, bf16[2,1,256,256]{3,2,1,0:T(8,128)(2,1)S(1)}, u32[]{:S(2)}, u32[]{:S(2)}) collective-permute-start(bf16[2,1,256,256]{3,2,1,0:T(8,128)(2,1)} %collective-permute-done.9), channel_id=1, source_target_pairs={{0,1},{1,0},{2,3},{3,2},{4,5},{5,4},{6,7},{7,6},{8,9},{9,8},{10,11... | collective-permute-start | bytes 786440 | tf_op jit(solution)/shard_map/ppermute | solution.py:129
  26.3 1.6 %copy-start = (bf16[2,8,256,256]{3,2,1,0:T(8,128)(2,1)S(1)}, bf16[2,8,256,256]{3,2,1,0:T(8,128)(2,1)}, u32[]{:S(2)}) copy-start(bf16[2,8,256,256]{3,2,1,0:T(8,128)(2,1)} %source.1) | copy-start | bytes 6291460
  27.9 0.7 %copy-start.2 = (s32[2,8]{1,0:T(2,128)S(1)}, s32[2,8]{1,0:T(2,128)}, u32[]{:S(2)}) copy-start(s32[2,8]{1,0:T(2,128)} %structure.9) | copy-start | bytes 196
  27.9 0.7 %copy-start.3 = (s32[16]{0:T(128)S(1)}, s32[16]{0:T(128)}, u32[]{:S(2)}) copy-start(s32[16]{0:T(128)} %block_slot.9) | copy-start | bytes 196
  30.2 1.8 %copy-start.1 = (bf16[2,1,256,256]{3,2,1,0:T(8,128)(2,1)S(1)}, bf16[2,1,256,256]{3,2,1,0:T(8,128)(2,1)}, u32[]{:S(2)}) copy-start(bf16[2,1,256,256]{3,2,1,0:T(8,128)(2,1)} %refs_0_.1) | copy-start | bytes 786436
  36.3 2.2 %copy-start.4 = (f32[2,256]{1,0:T(2,128)S(1)}, f32[2,256]{1,0:T(2,128)}, u32[]{:S(2)}) copy-start(f32[2,256]{1,0:T(2,128)} %diag.1) | copy-start | bytes 6148
  39.1 3.7 %collective-permute-start.12 = (f32[2,256]{1,0:T(2,128)S(1)}, f32[2,256]{1,0:T(2,128)S(1)}, u32[]{:S(2)}, u32[]{:S(2)}) collective-permute-start(f32[2,256]{1,0:T(2,128)S(1)} %get-tuple-element.25), channel_id=1, source_target_pairs={{0,2},{2,0},{4,6},{6,4},{8,10},{10,8},{12,14},{14,12},{1,3},{3,1},... | collective-permute-start | bytes 6152 | tf_op jit(solution)/shard_map/ppermute | solution.py:232
  42.7 3.6 %collective-permute-start.13 = (f32[2,256]{1,0:T(2,128)S(1)}, f32[2,256]{1,0:T(2,128)S(1)}, u32[]{:S(2)}, u32[]{:S(2)}) collective-permute-start(f32[2,256]{1,0:T(2,128)S(1)} %add.12), channel_id=1, source_target_pairs={{0,4},{2,6},{4,0},{6,2},{8,12},{10,14},{12,8},{14,10},{1,5},{3,7},... | collective-permute-start | bytes 6152 | tf_op jit(solution)/shard_map/ppermute | solution.py:232
  46.4 4.6 %collective-permute-start.14 = (f32[2,256]{1,0:T(2,128)S(1)}, f32[2,256]{1,0:T(2,128)S(1)}, u32[]{:S(2)}, u32[]{:S(2)}) collective-permute-start(f32[2,256]{1,0:T(2,128)S(1)} %add.13), channel_id=1, source_target_pairs={{0,8},{2,10},{4,12},{6,14},{8,0},{10,2},{12,4},{14,6},{1,9},{3,11}... | collective-permute-start | bytes 6152 | tf_op jit(solution)/shard_map/ppermute | solution.py:232

commit v4 on v3

--- a/solution.py
+++ b/solution.py
@@ -227,9 +227,16 @@
         name="store",
     )(sigma)
 
-    stride = 1
+    def swapped(x, stride):
+        return lax.ppermute(x, "prow", [(i, i ^ stride) for i in range(grid_rows)])
+
+    if grid_rows % 4 == 0:
+        value = (value + swapped(value, 1)) + (swapped(value, 2) + swapped(value, 3))
+        stride = 4
+    else:
+        stride = 1
     while stride < grid_rows:
-        value = value + lax.ppermute(value, "prow", [(i, i ^ stride) for i in range(grid_rows)])
+        value = value + swapped(value, stride)
         stride *= 2
     return sigma, value
 

time: 51.9 us -> 52.6 us (1.013)
  waiting for transfers between devices: 12.1 us -> 13.7 us
  starting transfers between devices: 24.7 us -> 23.7 us
    ppermute x3 -> x4, waiting for transfers between devices: 3.88 us -> 5.57 us  [swapped(): return lax.ppermute(x, 'prow', [(i, i ^ stride) for i in range(grid_rows)])]
    ppermute x3 -> x4, starting transfers between devices: 7.19 us -> 6.24 us  [swapped(): return lax.ppermute(x, 'prow', [(i, i ^ stride) for i in range(grid_rows)])]
  transfers between devices with their start and end apart: 15 -> 16, of which waited for: 10 -> 10; matrix products, arithmetic and copies ran while one was open for 0% -> 0% of each run, Pallas kernels for 21% -> 20%
where the time goes in v4:
time: 52.6 us; the launch traced here: 52.3 us
  starting transfers between devices  23.7 us (45%)
  waiting for transfers between devices  13.7 us (26%)
  Pallas kernels  11.3 us (21%)
  local copies, waits for them, and re-layouts  2.11 us (4%)
  between operations  0.8 us (2%)
  other arithmetic  0.59 us (1%)
    ppermute x7, starting transfers between devices, hop(): return lax.ppermute(x, AXES, pairs)  16.3 us
    ppermute x7, waiting for transfers between devices, hop(): return lax.ppermute(x, AXES, pairs)  6.86 us
    pallas_call x3, Pallas kernels, per_device(): pl.pallas_call(functools.partial(add_kernel, grid_rows, [k for k, _ in ba...  6.34 us
    ppermute x4, starting transfers between devices, swapped(): return lax.ppermute(x, 'prow', [(i, i ^ stride) for i in range(grid_rows)])  6.24 us
    ppermute x4, waiting for transfers between devices, swapped(): return lax.ppermute(x, 'prow', [(i, i ^ stride) for i in range(grid_rows)])  5.57 us
    pallas_call x2, Pallas kernels, per_device(): pl.pallas_call(functools.partial(prepare_kernel, grid_rows, sup, [k for k...  3.42 us
    unnamed x10, local copies, waits for them, and re-layouts  2.11 us
    ppermute x5, waiting for transfers between devices, cross(): return lax.ppermute(x, AXES, swap)  1.31 us
  transfers between devices with their start and end apart: 16, of which 10 were waited for; matrix products, arithmetic and copies ran while one was open for 0% of the time, Pallas kernels for 20%

profile of v4, /device:TPU:0, one launch (start us, length us, event | category | flops | bytes accessed | tf_op | source)
XLA Modules:
  0.0 52.3 jit_solution(2194229053078432087)
XLA Ops:
  0.6 0.6 %collective-permute-start = (bf16[2,8,256,256]{3,2,1,0:T(8,128)(2,1)}, bf16[2,8,256,256]{3,2,1,0:T(8,128)(2,1)}, u32[]{:S(2)}, u32[]{:S(2)}) collective-permute-start(bf16[2,8,256,256]{3,2,1,0:T(8,128)(2,1)} %source.1), channel_id=1, source_target_pairs={{0,1},{1,0},{2,3},{3,2},{4,5},{5,4},{6,7},{7,6},{8,9},{9,8},{10,11... | collective-permute-start | bytes 6291464 | tf_op jit(solution)/shard_map/ppermute | solution.py:129
  1.2 0.1 collective-permute-start.1
  1.3 3.0 %collective-permute-start.5 = (bf16[2,1,256,256]{3,2,1,0:T(8,128)(2,1)}, bf16[2,1,256,256]{3,2,1,0:T(8,128)(2,1)S(1)}, u32[]{:S(2)}, u32[]{:S(2)}) collective-permute-start(bf16[2,1,256,256]{3,2,1,0:T(8,128)(2,1)} %refs_0_.1), channel_id=1, source_target_pairs={{0,4},{1,3},{4,8},{5,1},{8,12},{9,5},{12,14},{13,9},{14,10},{15,13... | collective-permute-start | bytes 786440 | tf_op jit(solution)/shard_map/ppermute | solution.py:126
  4.3 1.3 %collective-permute-done.1 = bf16[2,1,256,256]{3,2,1,0:T(8,128)(2,1)S(1)} collective-permute-done((bf16[2,1,256,256]{3,2,1,0:T(8,128)(2,1)}, bf16[2,1,256,256]{3,2,1,0:T(8,128)(2,1)S(1)}, u32[]{:S(2)}, u32[]{:S(2)}) %collective-permute-start.1) | collective-permute-done | bytes 262176 | tf_op jit(solution)/shard_map/ppermute | solution.py:129
  5.6 2.9 %collective-permute-start.2 = (bf16[2,1,256,256]{3,2,1,0:T(8,128)(2,1)S(1)}, bf16[2,1,256,256]{3,2,1,0:T(8,128)(2,1)}, u32[]{:S(2)}, u32[]{:S(2)}) collective-permute-start(bf16[2,1,256,256]{3,2,1,0:T(8,128)(2,1)S(1)} %collective-permute-done.1), channel_id=1, source_target_pairs={{0,4},{1,3},{4,8},{5,1},{8,12},{9,5},{12,14},{13,9},{14,10},{15,13... | collective-permute-start | bytes 786440 | tf_op jit(solution)/shard_map/ppermute | solution.py:126
  8.5 0.3 collective-permute-done.5.refs_1_
  8.8 2.1 %collective-permute-start.6 = (bf16[2,1,256,256]{3,2,1,0:T(8,128)(2,1)S(1)}, bf16[2,1,256,256]{3,2,1,0:T(8,128)(2,1)S(1)}, u32[]{:S(2)}, u32[]{:S(2)}) collective-permute-start(bf16[2,1,256,256]{3,2,1,0:T(8,128)(2,1)S(1)} %collective-permute-done.5.refs_1_), channel_id=1, source_target_pairs={{0,4},{1,3},{4,8},{5,1},{8,12},{9,5},{12,14},{13,9},{14,10},{15,13... | collective-permute-start | bytes 786440 | tf_op jit(solution)/shard_map/ppermute | solution.py:126
  10.8 2.0 %collective-permute-done.2 = bf16[2,1,256,256]{3,2,1,0:T(8,128)(2,1)} collective-permute-done((bf16[2,1,256,256]{3,2,1,0:T(8,128)(2,1)S(1)}, bf16[2,1,256,256]{3,2,1,0:T(8,128)(2,1)}, u32[]{:S(2)}, u32[]{:S(2)}) %collective-permute-start.2) | collective-permute-done | bytes 262176 | tf_op jit(solution)/shard_map/ppermute | solution.py:126
  12.9 2.1 %collective-permute-start.3 = (bf16[2,1,256,256]{3,2,1,0:T(8,128)(2,1)}, bf16[2,1,256,256]{3,2,1,0:T(8,128)(2,1)}, u32[]{:S(2)}, u32[]{:S(2)}) collective-permute-start(bf16[2,1,256,256]{3,2,1,0:T(8,128)(2,1)} %collective-permute-done.2), channel_id=1, source_target_pairs={{0,4},{1,3},{4,8},{5,1},{8,12},{9,5},{12,14},{13,9},{14,10},{15,13... | collective-permute-start | bytes 786440 | tf_op jit(solution)/shard_map/ppermute | solution.py:126
  15.0 0.6 %collective-permute-done.6.refs_1_ = bf16[2,1,256,256]{3,2,1,0:T(8,128)(2,1)S(1)} collective-permute-done((bf16[2,1,256,256]{3,2,1,0:T(8,128)(2,1)S(1)}, bf16[2,1,256,256]{3,2,1,0:T(8,128)(2,1)S(1)}, u32[]{:S(2)}, u32[]{:S(2)}) %collective-permute-start.6) | collective-permute-done | bytes 262176 | tf_op jit(solution)/shard_map/ppermute | solution.py:126
  15.6 2.1 %collective-permute-start.7 = (bf16[2,1,256,256]{3,2,1,0:T(8,128)(2,1)S(1)}, bf16[2,1,256,256]{3,2,1,0:T(8,128)(2,1)S(1)}, u32[]{:S(2)}, u32[]{:S(2)}) collective-permute-start(bf16[2,1,256,256]{3,2,1,0:T(8,128)(2,1)S(1)} %collective-permute-done.6.refs_1_), channel_id=1, source_target_pairs={{0,4},{1,3},{4,8},{5,1},{8,12},{9,5},{12,14},{13,9},{14,10},{15,13... | collective-permute-start | bytes 786440 | tf_op jit(solution)/shard_map/ppermute | solution.py:126
  17.7 1.9 %collective-permute-done.3 = bf16[2,1,256,256]{3,2,1,0:T(8,128)(2,1)} collective-permute-done((bf16[2,1,256,256]{3,2,1,0:T(8,128)(2,1)}, bf16[2,1,256,256]{3,2,1,0:T(8,128)(2,1)}, u32[]{:S(2)}, u32[]{:S(2)}) %collective-permute-start.3) | collective-permute-done | bytes 262176 | tf_op jit(solution)/shard_map/ppermute | solution.py:126
  19.6 2.1 %collective-permute-start.9 = (bf16[2,1,256,256]{3,2,1,0:T(8,128)(2,1)}, bf16[2,1,256,256]{3,2,1,0:T(8,128)(2,1)}, u32[]{:S(2)}, u32[]{:S(2)}) collective-permute-start(bf16[2,1,256,256]{3,2,1,0:T(8,128)(2,1)} %collective-permute-done.3), channel_id=1, source_target_pairs={{0,4},{1,3},{4,8},{5,1},{8,12},{9,5},{12,14},{13,9},{14,10},{15,13... | collective-permute-start | bytes 786440 | tf_op jit(solution)/shard_map/ppermute | solution.py:126
  21.7 0.0 collective-permute-start.8
  21.7 0.5 collective-permute-start.4
  22.2 0.1 collective-permute-done.7.refs_1_
  22.3 2.1 %collective-permute-start.11 = (bf16[2,1,256,256]{3,2,1,0:T(8,128)(2,1)S(1)}, bf16[2,1,256,256]{3,2,1,0:T(8,128)(2,1)S(1)}, u32[]{:S(2)}, u32[]{:S(2)}) collective-permute-start(bf16[2,1,256,256]{3,2,1,0:T(8,128)(2,1)S(1)} %collective-permute-done.7.refs_1_), channel_id=1, source_target_pairs={{0,4},{1,3},{4,8},{5,1},{8,12},{9,5},{12,14},{13,9},{14,10},{15,13... | collective-permute-start | bytes 786440 | tf_op jit(solution)/shard_map/ppermute | solution.py:126
  24.4 1.9 %collective-permute-done.9 = bf16[2,1,256,256]{3,2,1,0:T(8,128)(2,1)} collective-permute-done((bf16[2,1,256,256]{3,2,1,0:T(8,128)(2,1)}, bf16[2,1,256,256]{3,2,1,0:T(8,128)(2,1)}, u32[]{:S(2)}, u32[]{:S(2)}) %collective-permute-start.9) | collective-permute-done | bytes 262176 | tf_op jit(solution)/shard_map/ppermute | solution.py:126
  26.3 0.0 collective-permute-start.10
  26.3 1.6 %copy-done = bf16[2,8,256,256]{3,2,1,0:T(8,128)(2,1)S(1)} copy-done((bf16[2,8,256,256]{3,2,1,0:T(8,128)(2,1)S(1)}, bf16[2,8,256,256]{3,2,1,0:T(8,128)(2,1)}, u32[]{:S(2)}) %copy-start) | copy-done | bytes 2097176
  27.9 0.1 load.1.own
  28.0 0.0 collective-permute-done.other
  28.0 0.5 copy-done.2
  28.5 0.0 copy-done.3
  28.5 1.7 %prepare.2 = (bf16[2,512,256]{2,1,0:T(8,128)(2,1)S(1)}, f32[6,256]{1,0:T(8,128)S(1)}) custom-call(s32[2,8]{1,0:T(2,128)S(1)} %copy-done.2, s32[16]{0:T(128)S(1)} %copy-done.3, bf16[2,8,256,256]{3,2,1,0:T(8,128)(2,1)S(1)} %load.1.own, bf16[2,8,256,256]{3,2,1,0:T(8,128)(2,1)} %collective-permute-done.other), custom_call_target="tpu_custom_call" | custom-call | bytes 1048576 | tf_op jit(solution)/shard_map/prepare/pallas_call | solution.py:185
  30.2 0.0 copy-start.1
  30.3 1.7 %prepare.3 = (bf16[2,512,256]{2,1,0:T(8,128)(2,1)S(1)}, f32[6,256]{1,0:T(8,128)S(1)}) custom-call(s32[2,8]{1,0:T(2,128)S(1)} %copy-done.2, s32[16]{0:T(128)S(1)} %copy-done.3, bf16[2,8,256,256]{3,2,1,0:T(8,128)(2,1)S(1)} %load.1.own, bf16[2,8,256,256]{3,2,1,0:T(8,128)(2,1)} %collective-permute-done.other), custom_call_target="tpu_custom_call" | custom-call | bytes 1048576 | tf_op jit(solution)/shard_map/prepare/pallas_call | solution.py:185
  32.0 0.0 copy-done.1
  32.0 2.1 %add.22 = (f32[2,512,256]{2,1,0:T(8,128)S(1)}, bf16[2,512,256]{2,1,0:T(8,128)(2,1)S(1)}) custom-call(s32[2,8]{1,0:T(2,128)S(1)} %copy-done.2, s32[16]{0:T(128)S(1)} %copy-done.3, bf16[2,8,256,256]{3,2,1,0:T(8,128)(2,1)S(1)} %load.1.own, bf16[2,8,256,256]{3,2,1,0:T(8,128)(2,1)} %collective-permute-done.other, bf16[2,1,256,256]{3,2,1,0:T(8,128)(2,1)S(1)} %copy-done.1, ...), custom_call_target="tpu_custom_call" | custom-call | flops 268435456 | bytes 1572864 | tf_op jit(solution)/shard_map/add/pallas_call | solution.py:166
  34.1 0.0 collective-permute-done.8.refs_0_
  34.1 2.1 %add.23 = (f32[2,512,256]{2,1,0:T(8,128)S(1)}, bf16[2,512,256]{2,1,0:T(8,128)(2,1)S(1)}) custom-call(s32[2,8]{1,0:T(2,128)S(1)} %copy-done.2, s32[16]{0:T(128)S(1)} %copy-done.3, bf16[2,8,256,256]{3,2,1,0:T(8,128)(2,1)S(1)} %load.1.own, bf16[2,8,256,256]{3,2,1,0:T(8,128)(2,1)} %collective-permute-done.other, ...), custom_call_target="tpu_custom_call", output_to_operand_aliasing={{0}: (6, {}), {1}: (7, {})} | custom-call | flops 268435456 | bytes 1572864 | tf_op jit(solution)/shard_map/add/pallas_call | solution.py:166
  36.3 0.0 collective-permute-done.4.refs_0_
  36.3 0.0 copy-start.4
  36.3 2.1 %add.24 = (f32[2,512,256]{2,1,0:T(8,128)S(1)}, bf16[2,512,256]{2,1,0:T(8,128)(2,1)S(1)}) custom-call(s32[2,8]{1,0:T(2,128)S(1)} %copy-done.2, s32[16]{0:T(128)S(1)} %copy-done.3, bf16[2,8,256,256]{3,2,1,0:T(8,128)(2,1)S(1)} %load.1.own, bf16[2,8,256,256]{3,2,1,0:T(8,128)(2,1)} %collective-permute-done.other, ...), custom_call_target="tpu_custom_call", output_to_operand_aliasing={{0}: (6, {}), {1}: (7, {})} | custom-call | flops 268435456 | bytes 1572864 | tf_op jit(solution)/shard_map/add/pallas_call | solution.py:166
  38.4 0.0 collective-permute-done.11.refs_5_
  38.4 0.0 collective-permute-done.10.refs_4_
  38.4 0.0 copy-done.4
  38.5 0.6 %finish.1 = (bf16[2,2,256,256]{3,2,1,0:T(8,128)(2,1)S(1)}, f32[2,256]{1,0:T(2,128)S(1)}) custom-call(f32[2,256]{1,0:T(2,128)S(1)} %copy-done.4, f32[1,256]{1,0:T(1,128)S(1)} %broadcast_in_dim.3.first, f32[2,512,256]{2,1,0:T(8,128)S(1)} %get-tuple-element.18.acc, bf16[2,512,256]{2,1,0:T(8,128)(2,1)S(1)} %get-tuple-element.19.own_panel, ...), custom_call_target="tpu_custom_call" | custom-call | flops 268435456 | bytes 2097152 | tf_op jit(solution)/shard_map/finish/pallas_call | solution.py:203
  39.1 2.1 %collective-permute-start.12 = (f32[2,256]{1,0:T(2,128)S(1)}, f32[2,256]{1,0:T(2,128)S(1)}, u32[]{:S(2)}, u32[]{:S(2)}) collective-permute-start(f32[2,256]{1,0:T(2,128)S(1)} %get-tuple-element.25), channel_id=1, source_target_pairs={{0,2},{2,0},{4,6},{6,4},{8,10},{10,8},{12,14},{14,12},{1,3},{3,1},... | collective-permute-start | bytes 6152 | tf_op jit(solution)/shard_map/ppermute | solution.py:231
  41.2 1.6 %collective-permute-start.13 = (f32[2,256]{1,0:T(2,128)S(1)}, f32[2,256]{1,0:T(2,128)S(1)}, u32[]{:S(2)}, u32[]{:S(2)}) collective-permute-start(f32[2,256]{1,0:T(2,128)S(1)} %get-tuple-element.25), channel_id=1, source_target_pairs={{0,4},{2,6},{4,0},{6,2},{8,12},{10,14},{12,8},{14,10},{1,5},{3,7},... | collective-permute-start | bytes 6152 | tf_op jit(solution)/shard_map/ppermute | solution.py:231
  42.7 0.0 collective-permute-start.14
  42.7 0.0 collective-permute-done.12
  42.8 2.0 %collective-permute-done.13 = f32[2,256]{1,0:T(2,128)S(1)} collective-permute-done((f32[2,256]{1,0:T(2,128)S(1)}, f32[2,256]{1,0:T(2,128)S(1)}, u32[]{:S(2)}, u32[]{:S(2)}) %collective-permute-start.13) | collective-permute-done | bytes 2080 | tf_op jit(solution)/shard_map/ppermute | solution.py:231
  44.8 2.5 %collective-permute-done.14 = f32[2,256]{1,0:T(2,128)S(1)} collective-permute-done((f32[2,256]{1,0:T(2,128)S(1)}, f32[2,256]{1,0:T(2,128)S(1)}, u32[]{:S(2)}, u32[]{:S(2)}) %collective-permute-start.14) | collective-permute-done | bytes 2080 | tf_op jit(solution)/shard_map/ppermute | solution.py:231
  47.2 2.6 %collective-permute-start.15 = (f32[2,256]{1,0:T(2,128)S(1)}, f32[2,256]{1,0:T(2,128)S(1)}, u32[]{:S(2)}, u32[]{:S(2)}) collective-permute-start(f32[2,256]{1,0:T(2,128)S(1)} %add_add_fusion), channel_id=1, source_target_pairs={{0,8},{2,10},{4,12},{6,14},{8,0},{10,2},{12,4},{14,6},{1,9},{3,11}... | collective-permute-start | bytes 6152 | tf_op jit(solution)/shard_map/ppermute | solution.py:231
  49.8 0.8 %store.1 = bf16[2,2,256,256]{3,2,1,0:T(8,128)(2,1)} custom-call(bf16[2,2,256,256]{3,2,1,0:T(8,128)(2,1)S(1)} %get-tuple-element.24.source), custom_call_target="tpu_custom_call" | custom-call | tf_op jit(solution)/shard_map/store/pallas_call | solution.py:220
  50.6 1.1 %collective-permute-done.15 = f32[2,256]{1,0:T(2,128)S(1)} collective-permute-done((f32[2,256]{1,0:T(2,128)S(1)}, f32[2,256]{1,0:T(2,128)S(1)}, u32[]{:S(2)}, u32[]{:S(2)}) %collective-permute-start.15) | collective-permute-done | bytes 2080 | tf_op jit(solution)/shard_map/ppermute | solution.py:231
  51.7 0.6 %add.18 = f32[2,256]{1,0:T(2,128)} add(f32[2,256]{1,0:T(2,128)S(1)} %add_add_fusion, f32[2,256]{1,0:T(2,128)S(1)} %collective-permute-done.15) | non-fusion elementwise | flops 512 | bytes 6144 | tf_op jit(solution)/shard_map/add | solution.py:239
  (5 shorter events, 0.0 us)
Async XLA Ops:
  0.6 27.4 %collective-permute-start = (bf16[2,8,256,256]{3,2,1,0:T(8,128)(2,1)}, bf16[2,8,256,256]{3,2,1,0:T(8,128)(2,1)}, u32[]{:S(2)}, u32[]{:S(2)}) collective-permute-start(bf16[2,8,256,256]{3,2,1,0:T(8,128)(2,1)} %source.1), channel_id=1, source_target_pairs={{0,1},{1,0},{2,3},{3,2},{4,5},{5,4},{6,7},{7,6},{8,9},{9,8},{10,11... | collective-permute-start | bytes 6291464 | tf_op jit(solution)/shard_map/ppermute | solution.py:129
  1.2 4.4 %collective-permute-start.1 = (bf16[2,1,256,256]{3,2,1,0:T(8,128)(2,1)}, bf16[2,1,256,256]{3,2,1,0:T(8,128)(2,1)S(1)}, u32[]{:S(2)}, u32[]{:S(2)}) collective-permute-start(bf16[2,1,256,256]{3,2,1,0:T(8,128)(2,1)} %refs_0_.1), channel_id=1, source_target_pairs={{0,1},{1,0},{2,3},{3,2},{4,5},{5,4},{6,7},{7,6},{8,9},{9,8},{10,11... | collective-permute-start | bytes 786440 | tf_op jit(solution)/shard_map/ppermute | solution.py:129
  1.3 7.5 %collective-permute-start.5 = (bf16[2,1,256,256]{3,2,1,0:T(8,128)(2,1)}, bf16[2,1,256,256]{3,2,1,0:T(8,128)(2,1)S(1)}, u32[]{:S(2)}, u32[]{:S(2)}) collective-permute-start(bf16[2,1,256,256]{3,2,1,0:T(8,128)(2,1)} %refs_0_.1), channel_id=1, source_target_pairs={{0,4},{1,3},{4,8},{5,1},{8,12},{9,5},{12,14},{13,9},{14,10},{15,13... | collective-permute-start | bytes 786440 | tf_op jit(solution)/shard_map/ppermute | solution.py:126
  5.6 7.3 %collective-permute-start.2 = (bf16[2,1,256,256]{3,2,1,0:T(8,128)(2,1)S(1)}, bf16[2,1,256,256]{3,2,1,0:T(8,128)(2,1)}, u32[]{:S(2)}, u32[]{:S(2)}) collective-permute-start(bf16[2,1,256,256]{3,2,1,0:T(8,128)(2,1)S(1)} %collective-permute-done.1), channel_id=1, source_target_pairs={{0,4},{1,3},{4,8},{5,1},{8,12},{9,5},{12,14},{13,9},{14,10},{15,13... | collective-permute-start | bytes 786440 | tf_op jit(solution)/shard_map/ppermute | solution.py:126
  8.8 6.8 %collective-permute-start.6 = (bf16[2,1,256,256]{3,2,1,0:T(8,128)(2,1)S(1)}, bf16[2,1,256,256]{3,2,1,0:T(8,128)(2,1)S(1)}, u32[]{:S(2)}, u32[]{:S(2)}) collective-permute-start(bf16[2,1,256,256]{3,2,1,0:T(8,128)(2,1)S(1)} %collective-permute-done.5.refs_1_), channel_id=1, source_target_pairs={{0,4},{1,3},{4,8},{5,1},{8,12},{9,5},{12,14},{13,9},{14,10},{15,13... | collective-permute-start | bytes 786440 | tf_op jit(solution)/shard_map/ppermute | solution.py:126
  12.9 6.7 %collective-permute-start.3 = (bf16[2,1,256,256]{3,2,1,0:T(8,128)(2,1)}, bf16[2,1,256,256]{3,2,1,0:T(8,128)(2,1)}, u32[]{:S(2)}, u32[]{:S(2)}) collective-permute-start(bf16[2,1,256,256]{3,2,1,0:T(8,128)(2,1)} %collective-permute-done.2), channel_id=1, source_target_pairs={{0,4},{1,3},{4,8},{5,1},{8,12},{9,5},{12,14},{13,9},{14,10},{15,13... | collective-permute-start | bytes 786440 | tf_op jit(solution)/shard_map/ppermute | solution.py:126
  15.6 6.7 %collective-permute-start.7 = (bf16[2,1,256,256]{3,2,1,0:T(8,128)(2,1)S(1)}, bf16[2,1,256,256]{3,2,1,0:T(8,128)(2,1)S(1)}, u32[]{:S(2)}, u32[]{:S(2)}) collective-permute-start(bf16[2,1,256,256]{3,2,1,0:T(8,128)(2,1)S(1)} %collective-permute-done.6.refs_1_), channel_id=1, source_target_pairs={{0,4},{1,3},{4,8},{5,1},{8,12},{9,5},{12,14},{13,9},{14,10},{15,13... | collective-permute-start | bytes 786440 | tf_op jit(solution)/shard_map/ppermute | solution.py:126
  19.6 6.7 %collective-permute-start.9 = (bf16[2,1,256,256]{3,2,1,0:T(8,128)(2,1)}, bf16[2,1,256,256]{3,2,1,0:T(8,128)(2,1)}, u32[]{:S(2)}, u32[]{:S(2)}) collective-permute-start(bf16[2,1,256,256]{3,2,1,0:T(8,128)(2,1)} %collective-permute-done.3), channel_id=1, source_target_pairs={{0,4},{1,3},{4,8},{5,1},{8,12},{9,5},{12,14},{13,9},{14,10},{15,13... | collective-permute-start | bytes 786440 | tf_op jit(solution)/shard_map/ppermute | solution.py:126
  21.7 12.5 %collective-permute-start.8 = (bf16[2,1,256,256]{3,2,1,0:T(8,128)(2,1)}, bf16[2,1,256,256]{3,2,1,0:T(8,128)(2,1)}, u32[]{:S(2)}, u32[]{:S(2)}) collective-permute-start(bf16[2,1,256,256]{3,2,1,0:T(8,128)(2,1)} %collective-permute-done.2), channel_id=1, source_target_pairs={{0,1},{1,0},{2,3},{3,2},{4,5},{5,4},{6,7},{7,6},{8,9},{9,8},{10,11... | collective-permute-start | bytes 786440 | tf_op jit(solution)/shard_map/ppermute | solution.py:129
  21.7 14.6 %collective-permute-start.4 = (bf16[2,1,256,256]{3,2,1,0:T(8,128)(2,1)}, bf16[2,1,256,256]{3,2,1,0:T(8,128)(2,1)}, u32[]{:S(2)}, u32[]{:S(2)}) collective-permute-start(bf16[2,1,256,256]{3,2,1,0:T(8,128)(2,1)} %collective-permute-done.3), channel_id=1, source_target_pairs={{0,1},{1,0},{2,3},{3,2},{4,5},{5,4},{6,7},{7,6},{8,9},{9,8},{10,11... | collective-permute-start | bytes 786440 | tf_op jit(solution)/shard_map/ppermute | solution.py:129
  22.3 16.1 %collective-permute-start.11 = (bf16[2,1,256,256]{3,2,1,0:T(8,128)(2,1)S(1)}, bf16[2,1,256,256]{3,2,1,0:T(8,128)(2,1)S(1)}, u32[]{:S(2)}, u32[]{:S(2)}) collective-permute-start(bf16[2,1,256,256]{3,2,1,0:T(8,128)(2,1)S(1)} %collective-permute-done.7.refs_1_), channel_id=1, source_target_pairs={{0,4},{1,3},{4,8},{5,1},{8,12},{9,5},{12,14},{13,9},{14,10},{15,13... | collective-permute-start | bytes 786440 | tf_op jit(solution)/shard_map/ppermute | solution.py:126
  26.3 12.2 %collective-permute-start.10 = (bf16[2,1,256,256]{3,2,1,0:T(8,128)(2,1)}, bf16[2,1,256,256]{3,2,1,0:T(8,128)(2,1)S(1)}, u32[]{:S(2)}, u32[]{:S(2)}) collective-permute-start(bf16[2,1,256,256]{3,2,1,0:T(8,128)(2,1)} %collective-permute-done.9), channel_id=1, source_target_pairs={{0,1},{1,0},{2,3},{3,2},{4,5},{5,4},{6,7},{7,6},{8,9},{9,8},{10,11... | collective-permute-start | bytes 786440 | tf_op jit(solution)/shard_map/ppermute | solution.py:129
  26.3 1.6 %copy-start = (bf16[2,8,256,256]{3,2,1,0:T(8,128)(2,1)S(1)}, bf16[2,8,256,256]{3,2,1,0:T(8,128)(2,1)}, u32[]{:S(2)}) copy-start(bf16[2,8,256,256]{3,2,1,0:T(8,128)(2,1)} %source.1) | copy-start | bytes 6291460
  27.9 0.7 %copy-start.2 = (s32[2,8]{1,0:T(2,128)S(1)}, s32[2,8]{1,0:T(2,128)}, u32[]{:S(2)}) copy-start(s32[2,8]{1,0:T(2,128)} %structure.9) | copy-start | bytes 196
  27.9 0.7 %copy-start.3 = (s32[16]{0:T(128)S(1)}, s32[16]{0:T(128)}, u32[]{:S(2)}) copy-start(s32[16]{0:T(128)} %block_slot.9) | copy-start | bytes 196
  30.2 1.8 %copy-start.1 = (bf16[2,1,256,256]{3,2,1,0:T(8,128)(2,1)S(1)}, bf16[2,1,256,256]{3,2,1,0:T(8,128)(2,1)}, u32[]{:S(2)}) copy-start(bf16[2,1,256,256]{3,2,1,0:T(8,128)(2,1)} %refs_0_.1) | copy-start | bytes 786436
  36.3 2.2 %copy-start.4 = (f32[2,256]{1,0:T(2,128)S(1)}, f32[2,256]{1,0:T(2,128)}, u32[]{:S(2)}) copy-start(f32[2,256]{1,0:T(2,128)} %diag.1) | copy-start | bytes 6148
  39.1 3.7 %collective-permute-start.12 = (f32[2,256]{1,0:T(2,128)S(1)}, f32[2,256]{1,0:T(2,128)S(1)}, u32[]{:S(2)}, u32[]{:S(2)}) collective-permute-start(f32[2,256]{1,0:T(2,128)S(1)} %get-tuple-element.25), channel_id=1, source_target_pairs={{0,2},{2,0},{4,6},{6,4},{8,10},{10,8},{12,14},{14,12},{1,3},{3,1},... | collective-permute-start | bytes 6152 | tf_op jit(solution)/shard_map/ppermute | solution.py:231
  41.2 3.6 %collective-permute-start.13 = (f32[2,256]{1,0:T(2,128)S(1)}, f32[2,256]{1,0:T(2,128)S(1)}, u32[]{:S(2)}, u32[]{:S(2)}) collective-permute-start(f32[2,256]{1,0:T(2,128)S(1)} %get-tuple-element.25), channel_id=1, source_target_pairs={{0,4},{2,6},{4,0},{6,2},{8,12},{10,14},{12,8},{14,10},{1,5},{3,7},... | collective-permute-start | bytes 6152 | tf_op jit(solution)/shard_map/ppermute | solution.py:231
  42.7 4.5 %collective-permute-start.14 = (f32[2,256]{1,0:T(2,128)S(1)}, f32[2,256]{1,0:T(2,128)S(1)}, u32[]{:S(2)}, u32[]{:S(2)}) collective-permute-start(f32[2,256]{1,0:T(2,128)S(1)} %get-tuple-element.25), channel_id=1, source_target_pairs={{0,6},{2,4},{4,2},{6,0},{8,14},{10,12},{12,10},{14,8},{1,7},{3,5},... | collective-permute-start | bytes 6152 | tf_op jit(solution)/shard_map/ppermute | solution.py:231
  47.2 4.5 %collective-permute-start.15 = (f32[2,256]{1,0:T(2,128)S(1)}, f32[2,256]{1,0:T(2,128)S(1)}, u32[]{:S(2)}, u32[]{:S(2)}) collective-permute-start(f32[2,256]{1,0:T(2,128)S(1)} %add_add_fusion), channel_id=1, source_target_pairs={{0,8},{2,10},{4,12},{6,14},{8,0},{10,2},{12,4},{14,6},{1,9},{3,11}... | collective-permute-start | bytes 6152 | tf_op jit(solution)/shard_map/ppermute | solution.py:231
